TPU v7x, 256 devices: a whole 4x4x8 slice. The times are simulated.
256 devices in a mesh: pair: 2 (over core), seq: 32 (over x, z), asset: 4 (over y).
Axes of the slice: x: 4, y: 4, z: 8, core: 2. Of those that a mesh axis runs over, the one named last changes fastest.
Arguments:
- latents: float32 [4, 8, 4096], P('asset', None, 'seq'), may hold values from -6 to 6
- voxel_coords: int32 [4, 3, 4096], P('asset', None, 'seq'), may hold values from 0 to 63
- owner_map: int32 [4, 4096, 1], P('asset', 'seq'), may hold values from 0 to 31; in each aligned block of 128 rows (0 to 127, 128 to 255, ..., all dimensions but the last counted through in order) at most 8 rows name the same one
- step_time: float32 [4], P('asset'), may hold values from 0.2 to 0.5
- modulation: float32 [4, 2, 5, 1024], P('asset', 'pair'), may hold values from -3 to 3
- in_proj: float32 [8, 1024], replicated, may hold values from -2 to 2
- qkv_proj: bfloat16 [1024, 1536], replicated, may hold values from -0.1875 to 0.1875
- norm_gain: float32 [2, 512], replicated, may hold values from 1.5 to 3
- out_proj: bfloat16 [512, 1024], replicated, may hold values from -0.25 to 0.25
- head_proj: float32 [1024, 8], replicated, may hold values from -0.1875 to 0.1875
- decoder_projection: float32 [8, 768], replicated, may hold values from -2 to 2
- border_blocks: int32 [4, 32, 2, 8], P('asset', 'seq'), may hold values from 0 to 15
- kernel_map: int32 [4, 32, 27, 1024], P('asset', 'seq'), may hold values from 0 to 512
- conv_weight: bfloat16 [27, 768, 192], P(None, None, 'pair'), may hold values from -0.0390625 to 0.0390625
Outputs:
- owned_latents: float32 [4, 32, 8, 256], P('asset', 'seq')
- decoded: bfloat16 [4, 32, 1024, 192], P('asset', 'seq', None, 'pair')
Inputs may be any that keep to these rules, and one draw needn't show every extreme that they name: `owner_map`: in each aligned block of 128 tokens (the tokens of one device) no owner is named by more than 8 tokens. `kernel_map`: rows below 256 are the owner's slots, the next 128 come from the owner below, the next 128 from the owner above, and 512 is the zero row.
All inputs are finite; a program needn't handle non-finite values.
Results may differ from a plain program's by a relative error of at most 0.0075.
Values may be sent and summed in bfloat16 or wider, within the bound.
A program may use at most 128 MiB of HBM per device.

v0:
```python
import math

import jax
import jax.numpy as jnp
from jax import lax
from jax.sharding import PartitionSpec as P

HEADS = 8
HEAD = 64
LAT = 8
BLK = 16


EPSILON = 1e-06
GUIDANCE = 3.0
TOP_PRECISION = lax.Precision.HIGHEST


def from_partner(shard, axis, apart):
    return lax.ppermute(shard, axis, [(i, i ^ 1 << apart) for i in range(lax.axis_size(axis))])


def extended(cells, sides, width):
    for axis, dim in sides:
        count = lax.axis_size(axis)
        ends = count - 1
        head = lax.slice_in_dim(cells, 0, width, axis=dim)
        tail = lax.slice_in_dim(cells, cells.shape[dim] - width, cells.shape[dim], axis=dim)
        cells = jnp.concatenate(
            [
                lax.ppermute(tail, axis, [(i, (i + 1) % count) for i in range(ends)]),
                cells,
                lax.ppermute(head, axis, [((i + 1) % count, i) for i in range(ends)]),
            ],
            axis=dim,
        )
    return cells


def layer_norm(values):
    center = values - jnp.mean(values, axis=-1, keepdims=True)
    variance = jnp.mean(center * center, axis=-1, keepdims=True)
    return center / jnp.sqrt(variance + EPSILON)


def position_table(coord_rows, model_width):
    freqs = model_width // 6
    steps = jnp.arange(freqs, dtype=jnp.float32) / freqs
    omegas = jnp.exp(-math.log(10000.0) * steps)
    angles = coord_rows.astype(jnp.float32)[:, :, None] * omegas[None, None, :]
    halves = jnp.concatenate([jnp.sin(angles), jnp.cos(angles)], axis=2)
    rows_out = jnp.transpose(halves, (1, 0, 2)).reshape(coord_rows.shape[1], 6 * freqs)
    return jnp.pad(rows_out, ((0, 0), (0, model_width - 6 * freqs)))


def head_norm(values, gains):
    row_count = values.shape[0]
    per_head = values.reshape(row_count, HEADS, HEAD)
    mean_square = jnp.mean(per_head * per_head, axis=2, keepdims=True)
    return (per_head / jnp.sqrt(mean_square + EPSILON)).reshape(row_count, HEADS * HEAD) * gains


def pack_slots(columns, owner_rows, seq_count, capacity):
    owner_ids = jnp.arange(seq_count, dtype=jnp.int32)
    onehot = (owner_rows[:, None] == owner_ids[None, :]).astype(jnp.int32)
    ranks = jnp.sum(onehot * (jnp.cumsum(onehot, axis=0) - 1), axis=1)
    slot_ids = owner_rows * capacity + ranks
    targets = jnp.arange(seq_count * capacity, dtype=jnp.int32)
    dispatch = (slot_ids[:, None] == targets[None, :]).astype(jnp.float32)
    packed = jnp.dot(columns, dispatch, precision=TOP_PRECISION)
    return packed.reshape(columns.shape[0], seq_count, capacity)


def per_device(
    latents,
    voxel_coords,
    owner_map,
    step_time,
    modulation,
    in_proj,
    qkv_proj,
    norm_gain,
    out_proj,
    head_proj,
    decoder_projection,
    border_blocks,
    kernel_map,
    conv_weight,
):
    latent_block = latents[0]
    token_count = latent_block.shape[1]
    model_width = in_proj.shape[1]
    inner_width = out_proj.shape[0]
    factor = HEAD ** (-0.5)
    mod_rows = modulation[0, 0]
    hidden = jnp.dot(latent_block.T, in_proj, precision=TOP_PRECISION) + position_table(
        voxel_coords[0], model_width
    )
    normed = (layer_norm(hidden) * (1.0 + mod_rows[1]) + mod_rows[0]).astype(jnp.bfloat16)
    projected = jnp.dot(normed, qkv_proj, preferred_element_type=jnp.float32)
    queries = head_norm(projected[:, :inner_width], norm_gain[0]).astype(jnp.bfloat16)
    keys_in = head_norm(projected[:, inner_width : 2 * inner_width], norm_gain[1]).astype(
        jnp.bfloat16
    )
    values_in = projected[:, 2 * inner_width :].astype(jnp.bfloat16)
    query_heads = queries.reshape(token_count, HEADS, HEAD)
    start_pair = (
        jnp.zeros((token_count, HEADS, HEAD), jnp.float32),
        jnp.zeros((token_count, HEADS), jnp.float32),
    )
    key_row_list = lax.all_gather(keys_in, "seq", axis=0, tiled=True)
    value_rows = lax.all_gather(values_in, "seq", axis=0, tiled=True)
    row_count = key_row_list.shape[0]
    block_rows = math.gcd(row_count, 512)
    key_blocks = key_row_list.reshape(row_count // block_rows, block_rows, HEADS, HEAD)
    value_blocks = value_rows.reshape(row_count // block_rows, block_rows, HEADS, HEAD)

    def one_block(running, block_pair):
        numer_run, denom_run = running
        key_block, value_block = block_pair
        scores = (
            jnp.einsum("qhd,khd->hqk", query_heads, key_block, preferred_element_type=jnp.float32)
            * factor
        )
        exp_scores = jnp.exp(scores)
        numer_run = numer_run + jnp.einsum(
            "hqk,khd->qhd",
            exp_scores.astype(jnp.bfloat16),
            value_block,
            preferred_element_type=jnp.float32,
        )
        denom_run = denom_run + jnp.sum(exp_scores, axis=2).T
        return ((numer_run, denom_run), None)

    result_pair, unused = lax.scan(one_block, start_pair, (key_blocks, value_blocks))
    numerator, denominator = result_pair
    attended = (
        (numerator / denominator[:, :, None]).reshape(token_count, inner_width).astype(jnp.bfloat16)
    )
    hidden = hidden + mod_rows[2] * jnp.dot(attended, out_proj, preferred_element_type=jnp.float32)
    final = layer_norm(hidden) * (1.0 + mod_rows[4]) + mod_rows[3]
    velocity = jnp.dot(final, head_proj, precision=TOP_PRECISION).T
    seq_count = lax.axis_size("seq")
    slot_count = kernel_map.shape[3] // 4
    capacity = slot_count // seq_count
    owner_rows = owner_map[0, :, 0]
    when_step = step_time[0]
    is_cond = lax.axis_index("pair") == 0
    partner = from_partner(velocity, "pair", 0)
    cond_velocity = jnp.where(is_cond, velocity, partner)
    uncond_velocity = jnp.where(is_cond, partner, velocity)
    clean = latent_block - when_step * (
        uncond_velocity + GUIDANCE * (cond_velocity - uncond_velocity)
    )
    packed = pack_slots(clean, owner_rows, seq_count, capacity)
    received = lax.all_to_all(packed, "seq", split_axis=1, concat_axis=1, tiled=True)
    owned_rows = received.reshape(LAT, slot_count)
    voxel_features = jax.nn.silu(
        jnp.dot(owned_rows.T, decoder_projection, precision=TOP_PRECISION)
    ).astype(jnp.bfloat16)
    block_count = slot_count // BLK
    chosen = border_blocks[0, 0].reshape(-1)
    halo_rows = border_blocks.shape[3] * BLK
    dec_width = decoder_projection.shape[1]
    tiles = voxel_features.reshape(block_count, BLK, dec_width)
    outgoing = jnp.take(tiles, chosen, axis=0).reshape(2 * halo_rows, dec_width)
    padded = extended(outgoing, (("seq", 0),), halo_rows)
    rim_features = jnp.concatenate([padded[:halo_rows], padded[-halo_rows:]], axis=0)
    zero_row = jnp.zeros((1, dec_width), jnp.bfloat16)
    rows_table = jnp.concatenate([voxel_features, rim_features, zero_row], axis=0)
    table_rows = rows_table.shape[0]
    products = jnp.einsum(
        "rc,kco->kro", rows_table, conv_weight, preferred_element_type=jnp.float32
    )
    row_ids = jnp.arange(table_rows, dtype=jnp.int32)
    index_maps = kernel_map[0, 0]
    fine_rows = index_maps.shape[1]

    def add_offset(total, offset_pair):
        product_rows, index_rows = offset_pair
        selector = (index_rows[:, None] == row_ids[None, :]).astype(jnp.float32)
        return (total + jnp.dot(selector, product_rows, precision=TOP_PRECISION), None)

    start_total = jnp.zeros((fine_rows, products.shape[2]), jnp.float32)
    summed, unused_rows = lax.scan(add_offset, start_total, (products, index_maps))
    decoded = summed.astype(jnp.bfloat16)
    return (owned_rows[None, None], decoded[None, None])


def solution(mesh):
    placed = (
        P("asset", None, "seq"),
        P("asset", None, "seq"),
        P("asset", "seq", None),
        P("asset"),
        P("asset", "pair", None, None),
        P(),
        P(),
        P(),
        P(),
        P(),
        P(),
        P("asset", "seq", None, None),
        P("asset", "seq", None, None),
        P(None, None, "pair"),
    )
    return jax.shard_map(
        per_device,
        mesh=mesh,
        in_specs=placed,
        out_specs=(P("asset", "seq", None, None), P("asset", "seq", None, "pair")),
        check_vma=False,
    )
```

profile of v0, /device:TPU:1, one launch (start us, length us, event | category | flops | bytes accessed | tf_op | source)
XLA Modules:
  0.0 400.6 jit_solution(336757916576435964)
XLA Ops:
  10.0 1.9 reshape.160
  11.8 2.0 copy.35
  13.9 1.7 fusion.58
  21.8 1.8 copy.40
  25.4 1.8 copy.41
  27.2 1.9 multiply_convert_fusion.1
  38.0 74.2 %all-gather.5.cloned.1.call-done = bf16[4096,512]{1,0:T(8,128)(2,1)} async-done(((bf16[128,512]{1,0:T(8,128)(2,1)}), bf16[4096,512]{1,0:T(8,128)(2,1)}) %all-gather.5.cloned.1.call-update) | async-done | bytes 4194320 | tf_op jit(solution)/shard_map/all_gather | solution.py:111
  112.2 11.2 %reshape.178 = bf16[8,512,8,64]{3,2,1,0:T(8,128)(2,1)} reshape(bf16[4096,512]{1,0:T(8,128)(2,1)} %all-gather.5.cloned.1.call-done) | data formatting | bytes 8388608 | tf_op jit(solution)/shard_map/reshape | solution.py:115
  123.4 9.8 %copy.44 = bf16[8,512,8,64]{1,3,2,0:T(8,128)(2,1)} copy(bf16[8,512,8,64]{3,2,1,0:T(8,128)(2,1)} %reshape.178) | data formatting | bytes 8388608
  133.2 61.2 %all-gather.3.cloned.1.call-done = bf16[4096,512]{1,0:T(8,128)(2,1)} async-done(((bf16[128,512]{1,0:T(8,128)(2,1)}), bf16[4096,512]{1,0:T(8,128)(2,1)}) %all-gather.3.cloned.1.call-update) | async-done | bytes 4194320 | tf_op jit(solution)/shard_map/all_gather | solution.py:112
  194.4 11.2 %reshape.177 = bf16[8,512,8,64]{3,2,1,0:T(8,128)(2,1)} reshape(bf16[4096,512]{1,0:T(8,128)(2,1)} %all-gather.3.cloned.1.call-done) | data formatting | bytes 8388608 | tf_op jit(solution)/shard_map/reshape | solution.py:116
  205.6 9.7 %copy.43 = bf16[8,512,8,64]{1,3,2,0:T(8,128)(2,1)} copy(bf16[8,512,8,64]{3,2,1,0:T(8,128)(2,1)} %reshape.177) | data formatting | bytes 8388608
  215.3 42.2 %while.24 = (s32[]{:T(128)}, f32[128,8,64]{0,2,1:T(8,128)S(1)}, f32[128,8]{0,1:T(8,128)S(1)}, bf16[8,512,8,64]{1,3,2,0:T(8,128)(2,1)}, bf16[8,512,8,64]{1,3,2,0:...) while((s32[]{:T(128)}, f32[128,8,64]{0,2,1:T(8,128)S(1)}, ...), condition=%wide.region_6.7_spmd.clone, body=%wide.region_4.6_spmd.clone.sunk | while | flops 136446976 | bytes 5915744 | solution.py:135
  215.3 2.9 bitcast_reduce_fusion.4
  218.3 2.3 fusion.76
  220.6 2.9 bitcast_reduce_fusion.4
  223.5 2.3 fusion.76
  225.9 2.9 bitcast_reduce_fusion.4
  228.8 2.3 fusion.76
  231.2 2.9 bitcast_reduce_fusion.4
  234.1 2.3 fusion.76
  236.4 2.9 bitcast_reduce_fusion.4
  239.4 2.3 fusion.76
  241.7 2.9 bitcast_reduce_fusion.4
  244.7 2.3 fusion.76
  247.0 2.9 bitcast_reduce_fusion.4
  249.9 2.3 fusion.76
  252.3 2.9 bitcast_reduce_fusion.4
  255.2 2.3 fusion.76
  257.7 1.8 fusion.59
  260.3 3.3 collective-permute-start
  265.6 5.5 %all-to-all-start = ((f32[8,32,8]{2,0,1:T(8,128)}), f32[8,32,8]{2,0,1:T(8,128)S(1)}, u32[]{:S(2)}, u32[]{:S(2)}) async-start(f32[8,32,8]{2,0,1:T(8,128)} %copy.45), calls=%async_computation | async-start | bytes 262144 | tf_op jit(solution)/shard_map/all_to_all | solution.py:156
  271.1 9.1 %all-to-all-done = f32[8,32,8]{2,0,1:T(8,128)S(1)} async-done(((f32[8,32,8]{2,0,1:T(8,128)}), f32[8,32,8]{2,0,1:T(8,128)S(1)}, u32[]{:S(2)}, u32[]{:S(2)}) %all-to-all-start) | async-done | bytes 8224 | tf_op jit(solution)/shard_map/all_to_all | solution.py:156
  284.6 3.6 collective-permute-start.1
  292.8 2.0 collective-permute-done.2
  294.9 8.6 %fusion.19 = f32[513,2592]{0,1} fusion(bf16[768,2592]{0,1:T(8,128)(2,1)} %bitcast.119, bf16[128,768]{1,0:T(8,128)(2,1)} %collective-permute-done.2, bf16[128,768]{1,0:T(8,128)(2,1)} %collective-permute-done.1, bf16[256,768]{1,0:T(8,128)(2,1)} %multiply_convert_fusion, bf16[513]{0:T(1024)(128)(2,1)S(1)} %pad.8.clone), kind=kOutput, calls=%fused_computation.29 | convolution fusion | flops 2045564928 | bytes 10087554
  303.5 89.6 %while.25 = (s32[]{:T(128)}, f32[1024,96]{0,1:T(8,128)S(1)}, s32[27,1024]{1,0:T(8,128)}, f32[27,513,96]{1,2,0:T(8,128)}, s32[]{:T(128)}, /*index=5*/s32[]{:T(128)}) while((s32[]{:T(128)}, f32[1024,96]{0,1:T(8,128)S(1)}, s32[27,1024]{1,0:T(8,128)}, f32[27,513,96]{1,2,0:T(8,128)}, s32[]{:T(128)}, /*index=5*/s32[]{:T(128)}) %tuple.75), condition=%wide.region_12.13_spmd.clone, body=%wide.region_11.12_spmd.clone.sunk | while | flops 605881344 | bytes 1045075 | solution.py:185
  304.2 2.5 fusion.78
  307.6 2.5 fusion.78
  310.9 2.5 fusion.78
  314.2 2.5 fusion.78
  317.5 2.5 fusion.78
  320.8 2.5 fusion.78
  324.1 2.5 fusion.78
  327.5 2.5 fusion.78
  330.8 2.5 fusion.78
  334.1 2.5 fusion.78
  337.4 2.5 fusion.78
  340.7 2.5 fusion.78
  344.1 2.5 fusion.78
  347.4 2.5 fusion.78
  350.7 2.5 fusion.78
  354.0 2.5 fusion.78
  357.3 2.5 fusion.78
  360.6 2.5 fusion.78
  364.0 2.5 fusion.78
  367.3 2.5 fusion.78
  370.6 2.5 fusion.78
  373.9 2.5 fusion.78
  377.2 2.5 fusion.78
  380.6 2.5 fusion.78
  383.9 2.5 fusion.78
  387.2 2.5 fusion.78
  390.5 2.5 fusion.78
  (128 shorter events, 52.0 us)
Async XLA Ops:
  7.2 9.3 %copy-start = (bf16[1024,1536]{1,0:T(8,128)(2,1)S(1)}, bf16[1024,1536]{1,0:T(8,128)(2,1)}, u32[]{:S(2)}) copy-start(bf16[1024,1536]{1,0:T(8,128)(2,1)} %param.24) | copy-start | bytes 9437188
  7.2 6.7 %copy-start.6 = (f32[1,8,128]{2,1,0:T(8,128)S(1)}, f32[1,8,128]{2,1,0:T(8,128)}, u32[]{:S(2)}) copy-start(f32[1,8,128]{2,1,0:T(8,128)} %param.18) | copy-start | bytes 12292
  7.2 6.7 %copy-start.4 = (f32[8,1024]{1,0:T(8,128)S(1)}, f32[8,1024]{1,0:T(8,128)}, u32[]{:S(2)}) copy-start(f32[8,1024]{1,0:T(8,128)} %param.23) | copy-start | bytes 98308
  7.2 8.7 %copy-start.5 = (f32[1,1,5,1024]{3,1,2,0:T(1,128)S(1)}, f32[1,1,5,1024]{3,1,2,0:T(1,128)}, u32[]{:S(2)}) copy-start(f32[1,1,5,1024]{3,1,2,0:T(1,128)} %param.22) | copy-start | bytes 61444
  7.2 105.0 %all-gather.5.cloned.1.call-start = ((), (), s32[]{:S(2)}) async-start(), calls=%async_computation.2 | async-start | bytes 4325376 | tf_op jit(solution)/shard_map/all_gather | solution.py:111
  15.6 3.3 copy-start.1
  17.1 0.9 copy-start.2
  18.0 9.2 %copy-start.9 = (f32[2,512]{1,0:T(2,128)S(1)}, f32[2,512]{1,0:T(2,128)}, u32[]{:S(2)}) copy-start(f32[2,512]{1,0:T(2,128)} %param.25) | copy-start | bytes 12292
  18.0 12.8 %copy-start.14 = (s32[1,1,2,8]{3,2,1,0:T(2,128)S(1)}, s32[1,1,2,8]{3,2,1,0:T(2,128)}, u32[]{:S(2)}) copy-start(s32[1,1,2,8]{3,2,1,0:T(2,128)} %param.29) | copy-start | bytes 196
  18.0 15.0 %copy-start.10 = (s32[1,128,1]{1,2,0:T(1,128)S(1)}, s32[1,128,1]{1,2,0:T(1,128)}, u32[]{:S(2)}) copy-start(s32[1,128,1]{1,2,0:T(1,128)} %param.20) | copy-start | bytes 1540
  29.1 165.2 %all-gather.3.cloned.1.call-start = ((), (), s32[]{:S(2)}) async-start(), calls=%async_computation.1 | async-start | bytes 4325376 | tf_op jit(solution)/shard_map/all_gather | solution.py:112
  257.6 2.1 copy-start.7
  257.6 2.1 copy-start.8
  257.6 2.1 copy-start.12
  257.6 6.1 %copy-start.16 = (s32[16]{0:T(128)S(1)}, s32[16]{0:T(128)}, u32[]{:S(2)}) copy-start(s32[16]{0:T(128)} %reshape_squeeze.5) | copy-start | bytes 196
  257.6 6.9 %copy-start.15 = (s32[128]{0:T(128)S(1)}, s32[128]{0:T(128)}, u32[]{:S(2)}) copy-start(s32[128]{0:T(128)} %multiply_add_fusion) | copy-start | bytes 1540
  257.6 13.5 %copy-start.11 = (s32[16]{0:T(128)S(1)}, s32[16]{0:T(128)}, u32[]{:S(2)}) copy-start(s32[16]{0:T(128)} %fusion.53) | copy-start | bytes 196
  257.6 22.8 %copy-start.13 = (f32[8,768]{1,0:T(8,128)S(1)}, f32[8,768]{1,0:T(8,128)}, u32[]{:S(2)}) copy-start(f32[8,768]{1,0:T(8,128)} %param.28) | copy-start | bytes 73732
  260.3 4.1 %collective-permute-start = (f32[8,128]{1,0:T(8,128)S(1)}, f32[8,128]{1,0:T(8,128)S(1)}, u32[]{:S(2)}, u32[]{:S(2)}) collective-permute-start(f32[8,128]{1,0:T(8,128)S(1)} %convolution_bitcast_fusion.1), channel_id=1, source_target_pairs={{0,128},{128,0},{1,129},{129,1},{2,130},{130,2},{3,131},{131,3},{4... | collective-permute-start | bytes 12296 | tf_op jit(solution)/shard_map/ppermute | solution.py:20
  265.6 14.7 %all-to-all-start = ((f32[8,32,8]{2,0,1:T(8,128)}), f32[8,32,8]{2,0,1:T(8,128)S(1)}, u32[]{:S(2)}, u32[]{:S(2)}) async-start(f32[8,32,8]{2,0,1:T(8,128)} %copy.45), calls=%async_computation | async-start | bytes 262144 | tf_op jit(solution)/shard_map/all_to_all | solution.py:156
  280.3 1.8 copy-start.3
  284.6 8.3 %collective-permute-start.1 = (bf16[128,768]{1,0:T(8,128)(2,1)}, bf16[128,768]{1,0:T(8,128)(2,1)}, u32[]{:S(2)}, u32[]{:S(2)}) collective-permute-start(bf16[128,768]{1,0:T(8,128)(2,1)} %bitcast.20), channel_id=1, source_target_pairs={{0,4},{4,8},{8,12},{12,16},{16,20},{20,24},{24,28},{28,32},{32,36}... | collective-permute-start | bytes 589832 | tf_op jit(solution)/shard_map/ppermute | solution.py:31
  288.2 6.7 %collective-permute-start.2 = (bf16[128,768]{1,0:T(8,128)(2,1)}, bf16[128,768]{1,0:T(8,128)(2,1)}, u32[]{:S(2)}, u32[]{:S(2)}) collective-permute-start(bf16[128,768]{1,0:T(8,128)(2,1)} %bitcast.21), channel_id=1, source_target_pairs={{4,0},{8,4},{12,8},{16,12},{20,16},{24,20},{28,24},{32,28},{36,32}... | collective-permute-start | bytes 589832 | tf_op jit(solution)/shard_map/ppermute | solution.py:33
Sparse Core Ops, SparseCore 0:
  29.3 82.8 all-gather.4
  115.3 78.9 all-gather.2
where the time goes:
time: 407 us; the launch traced here: 401 us
  waiting for transfers between devices  147 us (36%)
  matrix products  125 us (31%)
  local copies, waits for them, and re-layouts  85.1 us (21%)
  between operations  15.1 us (4%)
  starting transfers between devices  14 us (3%)
  other arithmetic  13.4 us (3%)
    all_gather x1, waiting for transfers between devices, per_device(): key_row_list = lax.all_gather(keys_in, 'seq', axis=0, tiled=True)  74.2 us
    dot_general x27, matrix products, add_offset(): jnp.dot(selector, product_rows, precision=TOP_PRECISION)  68.2 us
    all_gather x1, waiting for transfers between devices, per_device(): value_rows = lax.all_gather(values_in, 'seq', axis=0, tiled=True)  61.2 us
    dot_general x8, matrix products, one_block(): jnp.einsum('qhd,khd->hqk', query_heads, key_block, preferred_element_type...  23.5 us
    unnamed x38, local copies, waits for them, and re-layouts  22.1 us
    dynamic_slice x27, local copies, waits for them, and re-layouts, per_device(): lax.scan(add_offset, start_total, (products, index_maps))  20.7 us
    dot_general x8, matrix products, one_block(): jnp.einsum('hqk,khd->qhd', exp_scores.astype(jnp.bfloat16), value_block,...  18.4 us
    reshape x1, local copies, waits for them, and re-layouts, per_device(): key_row_list.reshape(row_count // block_rows, block_rows, HEADS, HEAD)  11.2 us
  transfers between devices with their start and end apart: 6, of which 5 were waited for; matrix products, arithmetic and copies ran while one was open for 8% of the time, Pallas kernels for 0%

commit v1 on v0

v1 whole, which is shorter than its diff:
```python
import math

import jax
import jax.numpy as jnp
import numpy as np
from jax import lax
from jax.experimental import pallas as pl
from jax.experimental.pallas import tpu as pltpu
from jax.sharding import PartitionSpec as P

D = 1024
HEADS = 8
HEAD = 64
LAT = 8
DEC = 768
KOFF = 27
BLK = 16
RES = 64
TOK = 128
CAP = 8
SLOTS = 256
HALO = 128
FINE = 1024
HW = 512
NX = 4
NZ = 8
N_SEQ = 32
OUT_DEV = 96
GROUP = NX * TOK
FEAT = 256
EPSILON = 1e-06
GUIDANCE = 3.0
LOG2E = 1.4426950408889634
HI = lax.Precision.HIGHEST
F32 = jnp.float32
BF16 = jnp.bfloat16


def centred_position_table():
    freqs = D // 6
    omegas = np.exp(-math.log(10000.0) * (np.arange(freqs) / freqs))
    angles = np.arange(RES)[:, None] * omegas[None, :]
    halves = np.concatenate([np.sin(angles), np.cos(angles)], axis=1)
    table = np.zeros((3 * RES, D))
    for axis in range(3):
        table[axis * RES : (axis + 1) * RES, axis * 2 * freqs : (axis + 1) * 2 * freqs] = halves
    return (table - table.mean(axis=1, keepdims=True)).astype(np.float32)


def split(values):
    high = values.astype(BF16)
    return high, (values - high.astype(F32)).astype(BF16)


def mm(a, b):
    return lax.dot_general(a, b, (((1,), (0,)), ((), ())), preferred_element_type=F32)


def mm_nt(a, b):
    return lax.dot_general(a, b, (((1,), (1,)), ((), ())), preferred_element_type=F32)


def mm3(a, b, product=mm):
    a_high, a_low = split(a)
    b_high, b_low = split(b)
    return product(a_high, b_high) + (product(a_high, b_low) + product(a_low, b_high))


def exact(a, b):
    return jnp.dot(a, b, precision=HI, preferred_element_type=F32)


def iota(shape, dim):
    return lax.broadcasted_iota(jnp.int32, shape, dim)


def one_hots(rows, width):
    ids = iota((RES, width), 0).astype(F32)
    return [jnp.where(ids == rows[c : c + 1, :], 1.0, 0.0) for c in range(3)]


def flow_kernel(
    lat_ref, coord_ref, own_ref, step_ref, mod_ref, inp_ref, gain_ref, head_ref, bb_ref, tab_ref, wqkv_hbm, wout_hbm,
    x_ref, nb_ref,
    gath, stage, wqkv, wout, bkt, bv_high, bv_low, gmat, umat, hid_ref, ft_ref, acc, rank_ref, headt, sendbuf, rbuf,
    lsem, xs_sem, xr_sem, zs_sem, zr_sem, as_sem, ar_sem,
):
    me = lax.axis_index("seq")
    pair = lax.axis_index("pair")
    x_me = me // NZ
    z_me = me % NZ

    def x_copy(shift):
        peer = ((x_me + shift) % NX) * NZ + z_me
        return pltpu.make_async_remote_copy(
            src_ref=gath.at[z_me, x_me], dst_ref=gath.at[z_me, x_me],
            send_sem=xs_sem.at[shift - 1], recv_sem=xr_sem.at[shift - 1],
            device_id={"seq": peer}, device_id_type=pl.DeviceIdType.MESH)

    def z_copy(shift):
        peer = x_me * NZ + (z_me + shift) % NZ
        return pltpu.make_async_remote_copy(
            src_ref=gath.at[z_me], dst_ref=gath.at[z_me],
            send_sem=zs_sem.at[shift - 1], recv_sem=zr_sem.at[shift - 1],
            device_id={"seq": peer}, device_id_type=pl.DeviceIdType.MESH)

    def a_copy(core, shift):
        dest = (me + shift) % N_SEQ
        return pltpu.make_async_remote_copy(
            src_ref=sendbuf.at[dest], dst_ref=rbuf.at[pair, me],
            send_sem=as_sem.at[core, shift], recv_sem=ar_sem.at[core, shift],
            device_id={"pair": (pair + core) % 2, "seq": dest}, device_id_type=pl.DeviceIdType.MESH)

    barrier = pltpu.get_barrier_semaphore()

    def greet(shift, carry):
        dest = (me + shift) % N_SEQ
        for core in range(2):
            @pl.when((shift > 0) | (core > 0))
            def _():
                pl.semaphore_signal(barrier, inc=1, device_id={"pair": (pair + core) % 2, "seq": dest},
                                    device_id_type=pl.DeviceIdType.MESH)
        return carry

    lax.fori_loop(0, N_SEQ, greet, 0)

    load_qkv = pltpu.make_async_copy(wqkv_hbm, wqkv, lsem.at[0])
    load_qkv.start()
    load_out = pltpu.make_async_copy(wout_hbm, wout, lsem.at[1])
    load_out.start()

    lat = lat_ref[...]
    stage[...] = jnp.zeros((16, TOK), F32)
    stage[0:8, :] = lat
    stage[8:11, :] = coord_ref[...].astype(F32)
    stage[11:13, 0:8] = bb_ref[...].astype(F32)
    packet = stage[...]
    gath[z_me, x_me] = packet.astype(BF16)

    lat_high = lat.astype(BF16).astype(F32)
    lat_low = lat - lat_high
    zero8 = jnp.zeros((8, TOK), F32)
    own_feat = jnp.concatenate(
        one_hots(packet[8:11, :], TOK) + [lat_high, zero8, lat_low, jnp.zeros((40, TOK), F32)], axis=0)
    own_feat = own_feat.T.astype(BF16)
    table = tab_ref[...]
    inp = inp_ref[...]
    inp = inp - jnp.mean(inp, axis=1, keepdims=True)
    basis = jnp.concatenate(
        [table, inp, jnp.zeros((8, D), F32), inp, jnp.zeros((40, D), F32)], axis=0)
    basis_high, basis_low = split(basis)
    hidden = mm(own_feat, basis_high) + mm(own_feat, basis_low)
    hid_ref[...] = hidden
    center = hidden - jnp.mean(hidden, axis=1, keepdims=True)
    variance = jnp.mean(center * center, axis=1, keepdims=True)
    scale1 = 1.0 + mod_ref[1:2, :]
    normed = (center * lax.rsqrt(variance + EPSILON) * scale1 + mod_ref[0:1, :]).astype(BF16)

    own_rows = jnp.broadcast_to(own_ref[...], (TOK, TOK)).astype(F32)
    own_cols = own_rows.T
    earlier = (own_rows == own_cols) & (iota((TOK, TOK), 1) < iota((TOK, TOK), 0))
    rank = jnp.sum(jnp.where(earlier, 1.0, 0.0), axis=1, keepdims=True)
    rank_ref[...] = jnp.where(rank == ((iota((TOK, TOK), 1) // LAT) % CAP).astype(F32), 1.0, 0.0)

    pl.semaphore_wait(barrier, 2 * N_SEQ - 1)
    for shift in range(1, NX):
        x_copy(shift).start()

    spread = jnp.where((iota((LAT, TOK), 1) % LAT) == iota((LAT, TOK), 0), 1.0, 0.0)
    headt[...] = exact(head_ref[...], spread)
    gram = mm_nt(basis_high, basis_high) + (mm_nt(basis_high, basis_low) + mm_nt(basis_low, basis_high))
    gram_high, gram_low = split(gram * (1.0 / D))
    gmat[0:FEAT, :] = gram_high
    gmat[FEAT : 2 * FEAT, :] = gram_low

    shift_rows = jnp.where(iota((8, D), 0) < 2, jnp.broadcast_to(mod_ref[0:1, :], (8, D)), 0.0)
    scaled = jnp.concatenate(
        [table * scale1, inp * scale1, shift_rows, jnp.zeros((48, D), F32)], axis=0)
    scaled_high, scaled_low = split(scaled)
    load_qkv.wait()
    keys_of = mm(scaled_high, wqkv[:, HW : 2 * HW]) + mm(scaled_low, wqkv[:, HW : 2 * HW])
    keys_t_high, keys_t_low = split(keys_of.T)
    bkt[...] = keys_t_high

    queries = mm(normed, wqkv[:, 0:HW])
    squares = queries * queries
    sq_high, sq_low = split(squares)
    per_head = jnp.where(iota((HW, HW), 0) // HEAD == iota((HW, HW), 1) // HEAD, 1.0 / HEAD, 0.0).astype(BF16)
    mean_sq = mm(sq_high, per_head) + mm(sq_low, per_head)
    queries = (queries * lax.rsqrt(mean_sq + EPSILON) * gain_ref[0:1, :]).astype(BF16).astype(F32)
    queries = queries * (gain_ref[1:2, :] * (HEAD ** (-0.5) * LOG2E))
    first_half = iota((TOK, 2 * HEAD), 1) < HEAD
    for two in range(HEADS // 2):
        columns = slice(two * 2 * HEAD, (two + 1) * 2 * HEAD)
        both = queries[:, columns]
        for odd in range(2):
            mine = jnp.where(first_half if odd == 0 else ~first_half, both, 0.0)
            q_high, q_low = split(mine)
            k_high, k_low = keys_t_high[columns, :], keys_t_low[columns, :]
            umat[2 * two + odd] = (mm(q_high, k_high) + (mm(q_high, k_low) + mm(q_low, k_high))).astype(BF16)

    for shift in range(1, NX):
        x_copy(shift).wait_recv()
    for shift in range(1, NZ):
        z_copy(shift).start()

    values_of = mm(scaled_high, wqkv[:, 2 * HW : 3 * HW]) + mm(scaled_low, wqkv[:, 2 * HW : 3 * HW])
    bv_high[...], bv_low[...] = split(values_of)
    acc[...] = jnp.zeros((HEADS, TOK, FEAT), F32)

    def one_group(step, carry):
        back = jnp.where(step % 2 == 0, (NZ - step // 2) % NZ, (step + 1) // 2)

        @pl.when(step > 0)
        def _():
            source = (z_me + NZ - back) % NZ
            pltpu.make_async_remote_copy(
                src_ref=gath.at[source], dst_ref=gath.at[source],
                send_sem=zs_sem.at[back - 1], recv_sem=zr_sem.at[back - 1],
                device_id={"seq": me}, device_id_type=pl.DeviceIdType.MESH).wait_recv()

        group = (z_me + NZ - back) % NZ
        rows = jnp.concatenate([gath[group, i].astype(F32) for i in range(NX)], axis=1)
        hots = one_hots(rows[8:11, :], GROUP)
        rest = jnp.concatenate([rows[0:8, :], jnp.zeros((56, GROUP), F32)], axis=0)
        plain = jnp.concatenate(hots + [rest], axis=0)
        plain_high = plain.astype(BF16)
        image = mm(gmat[0:FEAT, :], plain_high) + mm(gmat[FEAT : 2 * FEAT, :], plain_high)
        var_eps = jnp.sum(image * plain, axis=0, keepdims=True) + EPSILON
        std = jnp.sqrt(var_eps)
        log_std = (0.5 * LOG2E) * jnp.log(var_eps)
        std_high = std.astype(BF16).astype(F32)
        which = iota((8, GROUP), 0)
        std_rows = jnp.where(which == 0, std_high, jnp.where(which == 1, std - std_high, 0.0))
        rest = jnp.concatenate([rows[0:8, :], std_rows, jnp.zeros((48, GROUP), F32)], axis=0)
        ft_ref[0 : 3 * RES, :] = plain_high[0 : 3 * RES, :]
        ft_ref[3 * RES : FEAT, :] = rest.astype(BF16)
        for head in range(HEADS):
            keys_h = mm(bkt[head * HEAD : (head + 1) * HEAD, :], ft_ref[...])
            mean_h = jnp.sum(keys_h * keys_h, axis=0, keepdims=True) * (1.0 / HEAD)
            inv = lax.rsqrt(mean_h + EPSILON * var_eps)
            scores = mm(umat[head], ft_ref[...]) * inv - log_std
            weights = jnp.exp2(scores).astype(BF16)
            acc[head] += mm_nt(weights, ft_ref[...])
        return carry

    lax.fori_loop(0, NZ, one_group, 0)

    load_out.wait()
    lane = iota((TOK, FEAT), 1)
    pieces = []
    for two in range(HEADS // 2):
        columns = slice(two * 2 * HEAD, (two + 1) * 2 * HEAD)
        halves = []
        for odd in range(2):
            total = acc[2 * two + odd]
            denom = jnp.sum(jnp.where((lane == 200) | (lane == 201), total, 0.0), axis=1, keepdims=True)
            t_high, t_low = split(total * (1.0 / denom))
            halves.append(mm(t_high, bv_high[:, columns])
                          + (mm(t_low, bv_high[:, columns]) + mm(t_high, bv_low[:, columns])))
        pieces.append(jnp.where(first_half, halves[0], halves[1]))
    attended = jnp.concatenate(pieces, axis=1).astype(BF16)
    hidden = hid_ref[...] + mod_ref[2:3, :] * mm(attended, wout[...])
    center = hidden - jnp.mean(hidden, axis=1, keepdims=True)
    variance = jnp.mean(center * center, axis=1, keepdims=True)
    final = center * lax.rsqrt(variance + EPSILON) * (1.0 + mod_ref[4:5, :]) + mod_ref[3:4, :]
    velocity = mm3(final, headt[...])

    lat_cols = jnp.concatenate([lat_ref[...]] * (TOK // LAT), axis=0).T
    when_step = step_ref[0]
    is_cond = pair == 0
    share = jnp.where(is_cond, 1.0, 0.0) * lat_cols + (
        when_step * jnp.where(is_cond, -GUIDANCE, GUIDANCE - 1.0)) * velocity
    share = share * rank_ref[...]
    own32 = jnp.broadcast_to(own_ref[...], (N_SEQ, TOK))
    owner = iota((N_SEQ, TOK), 0)
    here = exact(jnp.where(own32 == owner, 1.0, 0.0), share)
    below = exact(jnp.where(own32 == owner - 1, 1.0, 0.0), share)
    above = exact(jnp.where(own32 == owner + 1, 1.0, 0.0), share)
    sendbuf[:, 0, :] = jnp.where(iota((N_SEQ, TOK), 1) < LAT * CAP, here, below)
    sendbuf[:, 1, :] = above

    keep = pltpu.make_async_copy(sendbuf.at[me], rbuf.at[pair, me], lsem.at[2])
    keep.start()

    def send(shift, carry):
        for core in range(2):
            @pl.when((shift > 0) | (core > 0))
            def _():
                a_copy(core, shift).start()
        return carry

    lax.fori_loop(0, N_SEQ, send, 0)

    lower = jnp.maximum(me - 1, 0)
    upper = jnp.minimum(me + 1, N_SEQ - 1)
    nb_ref[0:1, :] = gath[lower % NZ, lower // NZ].astype(F32)[12:13, :]
    nb_ref[1:2, :] = gath[upper % NZ, upper // NZ].astype(F32)[11:12, :]
    nb_ref[2:8, :] = jnp.zeros((6, TOK), F32)

    for shift in range(1, NX):
        x_copy(shift).wait_send()
    for shift in range(1, NZ):
        z_copy(shift).wait_send()

    def arrive(shift, carry):
        for core in range(2):
            @pl.when((shift > 0) | (core > 0))
            def _():
                source = (me + N_SEQ - shift) % N_SEQ
                pltpu.make_async_remote_copy(
                    src_ref=sendbuf.at[source], dst_ref=rbuf.at[(pair + core) % 2, source],
                    send_sem=as_sem.at[core, shift], recv_sem=ar_sem.at[core, shift],
                    device_id={"pair": pair, "seq": me}, device_id_type=pl.DeviceIdType.MESH).wait()
        return carry

    keep.wait()
    lax.fori_loop(0, N_SEQ, arrive, 0)
    x_ref[...] = rbuf[0] + rbuf[1]


def conv_kernel(x_ref, nb_ref, km_ref, dproj_ref, w_ref, owned_ref, dec_ref, feats, wpair, kmt, acc):
    x0 = x_ref[:, 0, :]
    x1 = x_ref[:, 1, :]

    slot = iota((N_SEQ, SLOTS), 1)
    pick = jnp.where(slot // CAP == iota((N_SEQ, SLOTS), 0), 1.0, 0.0)
    wide = lax.dot_general(x0, pick, (((0,), (0,)), ((), ())), precision=HI, preferred_element_type=F32)
    row = iota((TOK, SLOTS), 0)
    wide = jnp.where((iota((TOK, SLOTS), 1) % CAP == row // LAT), wide, 0.0)
    fold = jnp.where(iota((LAT, TOK), 1) % LAT == iota((LAT, TOK), 0), 1.0, 0.0)
    owned_ref[...] = exact(fold, wide)

    lane = iota((SLOTS, TOK), 1)
    own_rows = jnp.where(lane // LAT == iota((SLOTS, TOK), 0) // N_SEQ, jnp.concatenate([x0] * CAP, axis=0), 0.0)
    sub = iota((HALO, TOK), 0)
    lane = iota((HALO, TOK), 1)
    parts = [own_rows]
    for side, x_side in ((0, x0), (1, x1)):
        blocks = jnp.broadcast_to(nb_ref[side : side + 1, :], (HALO, TOK))
        chosen = jnp.sum(jnp.where(lane == sub // BLK, blocks, 0.0), axis=1, keepdims=True)
        source = chosen * (BLK // CAP) + ((iota((HALO, 1), 0) % BLK) // CAP).astype(F32)
        pick = jnp.where(iota((HALO, N_SEQ), 1).astype(F32) == source, 1.0, 0.0)
        rows = exact(pick, x_side)
        offset = CAP if side == 0 else 0
        parts.append(jnp.where(lane // LAT == sub % CAP + offset, rows, 0.0))
    latents = jnp.concatenate(parts, axis=0)
    proj = jnp.concatenate([dproj_ref[...]] * (TOK // LAT), axis=0)
    value = mm3(latents, proj)
    feats[...] = (value / (1.0 + jnp.exp(-value))).astype(BF16)

    kmt[...] = jnp.concatenate([km_ref[...].astype(F32), jnp.zeros((TOK - KOFF, FINE), F32)], axis=0).T
    acc[...] = jnp.zeros((FINE, TOK), F32)
    place = iota((1, 2 * SLOTS), 1)
    slots = jnp.where(place < SLOTS, (place % N_SEQ) * CAP + place // N_SEQ, place).astype(F32)
    for j in range(2):
        wpair[j] = jnp.zeros((DEC, 2 * TOK), BF16)

    def products(offset):
        wpair[0, :, 0:OUT_DEV] = w_ref[offset]
        return mm(feats[...], wpair[0, :, 0:TOK]).astype(BF16)

    def one_offset(offset, carry):
        prod = products(offset)
        for m in range(4):
            rows = slice(m * 256, (m + 1) * 256)
            index = kmt[rows, 0:1]
            hot = jnp.where(index == slots, 1.0, 0.0).astype(BF16)
            acc[rows, :] += mm(hot, prod)
        kmt[...] = pltpu.roll(kmt[...], TOK - 1, 1)
        return carry

    lax.fori_loop(0, KOFF, one_offset, 0)
    dec_ref[...] = acc[:, 0:OUT_DEV].astype(BF16)


def vmem(count):
    return [pl.BlockSpec(memory_space=pltpu.VMEM)] * count


def per_device(
    latents, voxel_coords, owner_map, step_time, modulation, in_proj, qkv_proj, norm_gain, out_proj, head_proj,
    decoder_projection, border_blocks, kernel_map, conv_weight,
):
    table = jnp.asarray(centred_position_table())
    dma = pltpu.SemaphoreType.DMA
    gathered, borders = pl.pallas_call(
        flow_kernel,
        out_shape=(jax.ShapeDtypeStruct((N_SEQ, 2, TOK), F32), jax.ShapeDtypeStruct((8, TOK), F32)),
        in_specs=vmem(3) + [pl.BlockSpec(memory_space=pltpu.SMEM)] + vmem(6) + [pl.BlockSpec(memory_space=pl.ANY)] * 2,
        out_specs=tuple(vmem(2)),
        scratch_shapes=[
            pltpu.VMEM((NZ, NX, 16, TOK), BF16),
            pltpu.VMEM((16, TOK), F32),
            pltpu.VMEM((D, 3 * HW), BF16),
            pltpu.VMEM((HW, D), BF16),
            pltpu.VMEM((HW, FEAT), BF16),
            pltpu.VMEM((FEAT, HW), BF16),
            pltpu.VMEM((FEAT, HW), BF16),
            pltpu.VMEM((2 * FEAT, FEAT), BF16),
            pltpu.VMEM((HEADS, TOK, FEAT), BF16),
            pltpu.VMEM((TOK, D), F32),
            pltpu.VMEM((FEAT, GROUP), BF16),
            pltpu.VMEM((HEADS, TOK, FEAT), F32),
            pltpu.VMEM((TOK, TOK), F32),
            pltpu.VMEM((D, TOK), F32),
            pltpu.VMEM((N_SEQ, 2, TOK), F32),
            pltpu.VMEM((2, N_SEQ, 2, TOK), F32),
            dma((3,)), dma((NX - 1,)), dma((NX - 1,)), dma((NZ - 1,)), dma((NZ - 1,)),
            dma((2, N_SEQ)), dma((2, N_SEQ)),
        ],
        compiler_params=pltpu.CompilerParams(collective_id=0, has_side_effects=True, vmem_limit_bytes=40 << 20),
        name="flow",
    )(
        latents[0], voxel_coords[0], owner_map.reshape(1, TOK), step_time, modulation[0, 0], in_proj, norm_gain,
        head_proj, border_blocks[0, 0], table, qkv_proj, out_proj,
    )
    owned, decoded = pl.pallas_call(
        conv_kernel,
        out_shape=(jax.ShapeDtypeStruct((LAT, SLOTS), F32), jax.ShapeDtypeStruct((FINE, OUT_DEV), BF16)),
        in_specs=vmem(5),
        out_specs=tuple(vmem(2)),
        scratch_shapes=[
            pltpu.VMEM((2 * SLOTS, DEC), BF16),
            pltpu.VMEM((2, DEC, 2 * TOK), BF16),
            pltpu.VMEM((FINE, TOK), F32),
            pltpu.VMEM((FINE, TOK), F32),
        ],
        compiler_params=pltpu.CompilerParams(vmem_limit_bytes=40 << 20),
        name="conv",
    )(gathered, borders, kernel_map[0, 0], decoder_projection, conv_weight)
    return owned[None, None], decoded[None, None]


def solution(mesh):
    placed = (
        P("asset", None, "seq"),
        P("asset", None, "seq"),
        P("asset", "seq", None),
        P("asset"),
        P("asset", "pair", None, None),
        P(),
        P(),
        P(),
        P(),
        P(),
        P(),
        P("asset", "seq", None, None),
        P("asset", "seq", None, None),
        P(None, None, "pair"),
    )
    return jax.shard_map(
        per_device,
        mesh=mesh,
        in_specs=placed,
        out_specs=(P("asset", "seq", None, None), P("asset", "seq", None, "pair")),
        check_vma=False,
    )
```

time: 407 us -> 94.5 us (0.23); the launches traced: 401 us -> 93.8 us
  waiting for transfers between devices: 147 us -> 0 us
  matrix products: 125 us -> 0 us
  Pallas kernels: 0 us -> 71.6 us
  local copies, waits for them, and re-layouts: 85.1 us -> 20.9 us
  starting transfers between devices: 14 us -> 0 us
  between operations: 15.1 us -> 1.33 us
  other arithmetic: 13.4 us -> 0 us
    all_gather x2 -> x0, waiting for transfers between devices: 135 us -> none  [the longest x1 74.2 us: per_device(): key_row_list = lax.all_gather(keys_in, 'seq', axis=0, tiled=True)]
    dot_general x49 -> x0, matrix products: 117 us -> none  [the longest x27 68.2 us: add_offset(): jnp.dot(selector, product_rows, precision=TOP_PRECISION)]
    pallas_call x0 -> x2, Pallas kernels: none -> 71.6 us  [the longest x1 40 us: per_device(): pl.pallas_call(flow_kernel, out_shape=(jax.ShapeDtypeStruct((N_SEQ, 2, TO...]
    reshape x7 -> x0, local copies, waits for them, and re-layouts: 27.3 us -> none  [the longest x1 11.2 us: per_device(): key_row_list.reshape(row_count // block_rows, block_rows, HEADS, HEAD)]
    dynamic_slice x27 -> x0, local copies, waits for them, and re-layouts: 20.7 us -> none  [per_device(): lax.scan(add_offset, start_total, (products, index_maps))]
    all_to_all x1 -> x0, waiting for transfers between devices: 9.13 us -> none  [per_device(): lax.all_to_all(packed, 'seq', split_axis=1, concat_axis=1, tiled=True)]
    unnamed x1 -> x0, matrix products: 8.59 us -> none
    ppermute x3 -> x0, starting transfers between devices: 8.39 us -> none  [the longest x1 3.61 us: extended(): lax.ppermute(tail, axis, [(i, (i + 1) % count) for i in range(ends)])]
  transfers between devices with their start and end apart: 6 -> 0, of which waited for: 5 -> 0; matrix products, arithmetic and copies ran while one was open for 8% -> 0% of each run, Pallas kernels for 0% -> 0%
where the time goes in v1:
time: 94.5 us; the launch traced here: 93.8 us
  Pallas kernels  71.6 us (76%)
  local copies, waits for them, and re-layouts  20.9 us (22%)
  between operations  1.33 us (1%)
    pallas_call x1, Pallas kernels, per_device(): pl.pallas_call(flow_kernel, out_shape=(jax.ShapeDtypeStruct((N_SEQ, 2, TO...  40 us
    pallas_call x1, Pallas kernels, per_device(): pl.pallas_call(conv_kernel, out_shape=(jax.ShapeDtypeStruct((LAT, SLOTS),...  31.6 us
    unnamed x26, local copies, waits for them, and re-layouts  20.9 us

profile of v1, /device:TPU:1, one launch (start us, length us, event | category | flops | bytes accessed | tf_op | source)
XLA Modules:
  0.0 93.8 jit_solution(3700899794251814740)
XLA Ops:
  1.3 0.7 copy.28
  2.0 0.7 copy.27
  2.7 0.9 copy.26
  3.6 1.0 %copy.17.head_ref = f32[1024,8]{1,0:T(8,128)S(1)} copy(f32[1024,8]{0,1:T(8,128)} %param.24) | data formatting | bytes 65536 | tf_op args[9]
  4.6 0.0 copy-start.1
  4.6 1.9 %copy-done.1 = bf16[1024,1536]{1,0:T(8,128)(2,1)S(1)} copy-done((bf16[1024,1536]{1,0:T(8,128)(2,1)S(1)}, bf16[1024,1536]{1,0:T(8,128)(2,1)}, u32[]{:S(2)}) %copy-start.1) | copy-done | bytes 3145752
  6.5 0.0 copy-start.2
  6.5 1.2 %copy-done.2 = bf16[512,1024]{1,0:T(8,128)(2,1)S(1)} copy-done((bf16[512,1024]{1,0:T(8,128)(2,1)S(1)}, bf16[512,1024]{1,0:T(8,128)(2,1)}, u32[]{:S(2)}) %copy-start.2) | copy-done | bytes 1048600
  7.7 0.0 copy-start.3
  7.7 1.1 %copy-done.3 = f32[192,1024]{1,0:T(8,128)S(1)} copy-done((f32[192,1024]{1,0:T(8,128)S(1)}, f32[192,1024]{1,0:T(8,128)}, u32[]{:S(2)}) %copy-start.3) | copy-done | bytes 786456
  8.8 0.0 copy-start.4
  8.8 0.8 copy-done.4
  9.6 0.0 copy-start.6
  9.6 0.7 copy-done.6
  10.3 0.0 copy-start.7
  10.3 0.7 copy-done.7
  11.0 0.0 copy-start.8
  11.0 0.7 copy-done.8
  11.6 0.0 copy-start.9
  11.6 0.7 copy-done.9
  12.3 40.0 %flow.1 = (f32[32,2,128]{2,1,0:T(2,128)S(1)}, f32[8,128]{1,0:T(8,128)S(1)}) custom-call(f32[8,128]{1,0:T(8,128)S(1)} %bitcast.18, s32[3,128]{1,0:T(4,128)S(1)} %bitcast.17, s32[1,128]{1,0:T(1,128)S(1)} %bitcast.20, f32[1]{0:T(128)S(6)} %copy.29.step_ref, f32[5,1024]{1,0:T(8,128)S(1)} %bitcast.16, f32[8,1024]{1,0:T(8,128)S(1)} %copy-done.4, ...), custom_call_target="tpu_custom_call" | custom-call | tf_op jit(solution)/shard_map/flow/pallas_call | solution.py:387
  52.3 0.0 copy-start.5
  52.3 6.6 %copy.18.w_ref = bf16[27,768,96]{2,1,0:T(8,128)(2,1)} copy(bf16[27,768,96]{1,2,0:T(8,128)(2,1)} %param.28) | data formatting | bytes 7962624 | tf_op args[13]
  58.9 0.0 copy-done.5
  58.9 0.0 copy-start
  58.9 2.5 %copy-done = bf16[27,768,96]{2,1,0:T(8,128)(2,1)S(1)} copy-done((bf16[27,768,96]{2,1,0:T(8,128)(2,1)S(1)}, bf16[27,768,96]{2,1,0:T(8,128)(2,1)}, u32[]{:S(2)}) %copy-start) | copy-done | bytes 3981336
  61.4 31.6 %conv.1 = (f32[8,256]{1,0:T(8,128)}, bf16[1024,96]{1,0:T(8,128)(2,1)S(1)}) custom-call(f32[32,2,128]{2,1,0:T(2,128)S(1)} %get-tuple-element.6.x_ref, f32[8,128]{1,0:T(8,128)S(1)} %get-tuple-element.7.nb_ref, s32[27,1024]{1,0:T(8,128)S(1)} %bitcast.14, f32[8,768]{1,0:T(8,128)S(1)} %copy-done.5, bf16[27,768,96]{2,1,0:T(8,128)(2,1)S(1)} %copy-done), custom_call_target="tpu_custom_call" | custom-call | tf_op jit(solution)/shard_map/conv/pallas_call | solution.py:418
  93.0 0.8 copy.19
Async XLA Ops:
  4.6 1.9 %copy-start.1 = (bf16[1024,1536]{1,0:T(8,128)(2,1)S(1)}, bf16[1024,1536]{1,0:T(8,128)(2,1)}, u32[]{:S(2)}) copy-start(bf16[1024,1536]{1,0:T(8,128)(2,1)} %wqkv_hbm.1) | copy-start | bytes 9437188
  6.5 1.2 %copy-start.2 = (bf16[512,1024]{1,0:T(8,128)(2,1)S(1)}, bf16[512,1024]{1,0:T(8,128)(2,1)}, u32[]{:S(2)}) copy-start(bf16[512,1024]{1,0:T(8,128)(2,1)} %wout_hbm.1) | copy-start | bytes 3145732
  7.7 1.1 %copy-start.3 = (f32[192,1024]{1,0:T(8,128)S(1)}, f32[192,1024]{1,0:T(8,128)}, u32[]{:S(2)}) copy-start(f32[192,1024]{1,0:T(8,128)} %constant.2.clone.tab_ref) | copy-start | bytes 2359300
  8.8 0.8 copy-start.4
  9.6 0.7 copy-start.6
  10.3 0.7 copy-start.7
  11.0 0.7 copy-start.8
  11.6 0.7 copy-start.9
  52.3 6.6 %copy-start.5 = (f32[8,768]{1,0:T(8,128)S(1)}, f32[8,768]{1,0:T(8,128)}, u32[]{:S(2)}) copy-start(f32[8,768]{1,0:T(8,128)} %dproj_ref.1) | copy-start | bytes 73732
  58.9 2.5 %copy-start = (bf16[27,768,96]{2,1,0:T(8,128)(2,1)S(1)}, bf16[27,768,96]{2,1,0:T(8,128)(2,1)}, u32[]{:S(2)}) copy-start(bf16[27,768,96]{2,1,0:T(8,128)(2,1)} %copy.18.w_ref) | copy-start | bytes 11943940

commit v2 on v1

v2 whole, which is shorter than its diff:
```python
import math

import jax
import jax.numpy as jnp
import numpy as np
from jax import lax
from jax.experimental import pallas as pl
from jax.experimental.pallas import tpu as pltpu
from jax.sharding import PartitionSpec as P

D = 1024
HEADS = 8
HEAD = 64
LAT = 8
DEC = 768
KOFF = 27
BLK = 16
RES = 64
TOK = 128
CAP = 8
SLOTS = 256
HALO = 128
FINE = 1024
HW = 512
NX = 4
NZ = 8
N_SEQ = 32
OUT_DEV = 96
GROUP = NX * TOK
FEAT = 256
EPSILON = 1e-06
GUIDANCE = 3.0
LOG2E = 1.4426950408889634
HI = lax.Precision.HIGHEST
F32 = jnp.float32
BF16 = jnp.bfloat16


def centred_position_table():
    freqs = D // 6
    omegas = np.exp(-math.log(10000.0) * (np.arange(freqs) / freqs))
    angles = np.arange(RES)[:, None] * omegas[None, :]
    halves = np.concatenate([np.sin(angles), np.cos(angles)], axis=1)
    table = np.zeros((3 * RES, D))
    for axis in range(3):
        table[axis * RES : (axis + 1) * RES, axis * 2 * freqs : (axis + 1) * 2 * freqs] = halves
    return (table - table.mean(axis=1, keepdims=True)).astype(np.float32)


def split(values):
    high = values.astype(BF16)
    return high, (values - high.astype(F32)).astype(BF16)


def mm(a, b):
    return lax.dot_general(a, b, (((1,), (0,)), ((), ())), preferred_element_type=F32)


def mm_nt(a, b):
    return lax.dot_general(a, b, (((1,), (1,)), ((), ())), preferred_element_type=F32)


def mm3(a, b, product=mm):
    a_high, a_low = split(a)
    b_high, b_low = split(b)
    return product(a_high, b_high) + (product(a_high, b_low) + product(a_low, b_high))


def exact(a, b):
    return jnp.dot(a, b, precision=HI, preferred_element_type=F32)


def iota(shape, dim):
    return lax.broadcasted_iota(jnp.int32, shape, dim)


def one_hots(rows, width):
    ids = iota((RES, width), 0).astype(F32)
    return [jnp.where(ids == rows[c : c + 1, :], 1.0, 0.0) for c in range(3)]


def flow_kernel(
    lat_hbm, coord_hbm, own_hbm, step_ref, mod_hbm, inp_hbm, gain_hbm, head_hbm, bb_hbm, tabh_hbm, tabl_hbm, wqkv_hbm,
    wout_hbm,
    x_ref, nb_ref,
    lat_ref, coord_ref, own_ref, mod_ref, inp_ref, gain_ref, head_ref, bb_ref, tabh, tabl, wqkv, wout,
    gath, stage, bkt, bv_high, bv_low, umat, hid_ref, ft_ref, p_ref, acc, vel_ref, vel_in, sendbuf, rbuf,
    lsem, gs_sem, gr_sem, ps_sem, pr_sem, as_sem, ar_sem,
):
    me = lax.axis_index("seq")
    pair = lax.axis_index("pair")
    other = 1 - pair
    x_me = me // NZ
    z_me = me % NZ
    mesh_ids = pl.DeviceIdType.MESH

    barrier = pltpu.get_barrier_semaphore()
    for shift in range(1, N_SEQ):
        pl.semaphore_signal(barrier, inc=1, device_id={"seq": (me + shift) % N_SEQ}, device_id_type=mesh_ids)
    pl.semaphore_signal(barrier, inc=1, device_id={"pair": other}, device_id_type=mesh_ids)

    loads = [
        pltpu.make_async_copy(source, target, lsem.at[number])
        for number, (source, target) in enumerate((
            (lat_hbm, lat_ref), (coord_hbm, coord_ref), (own_hbm, own_ref), (mod_hbm, mod_ref), (inp_hbm, inp_ref),
            (gain_hbm, gain_ref), (head_hbm, head_ref), (bb_hbm, bb_ref), (tabh_hbm, tabh), (tabl_hbm, tabl),
            (wqkv_hbm, wqkv), (wout_hbm, wout)))
    ]
    for load in loads:
        load.start()
    for load in loads[:10]:
        load.wait()

    lat = lat_ref[...]
    stage[...] = jnp.zeros((16, TOK), F32)
    stage[0:8, :] = lat
    for axis in range(3):
        stage[8 + axis : 9 + axis, :] = coord_ref[axis].astype(F32)
    stage[11:12, 0:8] = bb_ref[0:1, :].astype(F32)
    stage[11:12, 8:16] = bb_ref[1:2, :].astype(F32)
    lat_high = lat.astype(BF16).astype(F32)
    zero8 = jnp.zeros((8, TOK), F32)
    own_feat = jnp.concatenate(
        one_hots(stage[8:11, :], TOK) + [lat_high, zero8, lat - lat_high, jnp.zeros((40, TOK), F32)], axis=0)
    own_feat = own_feat.T.astype(BF16)
    inp = inp_ref[...]
    inp = inp - jnp.mean(inp, axis=1, keepdims=True)
    inp_rows = jnp.concatenate([inp, jnp.zeros((8, D), F32), inp, jnp.zeros((40, D), F32)], axis=0)
    rows_high, rows_low = split(inp_rows)
    basis_high = jnp.concatenate([tabh[...], rows_high], axis=0)
    basis_low = jnp.concatenate([tabl[...], rows_low], axis=0)
    hidden = mm(own_feat, basis_high) + mm(own_feat, basis_low)
    hid_ref[...] = hidden
    center = hidden - jnp.mean(hidden, axis=1, keepdims=True)
    variance = jnp.mean(center * center, axis=1, keepdims=True)
    std = jnp.broadcast_to(jnp.sqrt(variance + EPSILON), (TOK, TOK)).T[0:1, :]
    std_high = std.astype(BF16).astype(F32)
    stage[12:13, :] = std_high
    stage[13:14, :] = std - std_high
    gath[me] = stage[...].astype(BF16)

    def g_copy(shift):
        return pltpu.make_async_remote_copy(
            src_ref=gath.at[me], dst_ref=gath.at[me], send_sem=gs_sem.at[shift], recv_sem=gr_sem.at[shift],
            device_id={"seq": (me + shift) % N_SEQ}, device_id_type=mesh_ids)

    pl.semaphore_wait(barrier, N_SEQ)
    for shift in range(1, N_SEQ):
        g_copy(shift).start()

    scale1 = 1.0 + mod_ref[1]
    normed = (center * lax.rsqrt(variance + EPSILON) * scale1 + mod_ref[0]).astype(BF16)
    shift_rows = jnp.where(iota((8, D), 0) < 2, jnp.broadcast_to(mod_ref[0], (8, D)), 0.0)
    scaled = jnp.concatenate(
        [(tabh[...].astype(F32) + tabl[...].astype(F32)) * scale1, inp * scale1, shift_rows, jnp.zeros((48, D), F32)],
        axis=0)
    scaled_high, scaled_low = split(scaled)
    loads[10].wait()
    keys_of = mm(scaled_high, wqkv[:, HW : 2 * HW]) + mm(scaled_low, wqkv[:, HW : 2 * HW])
    keys_t_high, keys_t_low = split(keys_of.T)
    bkt[...] = keys_t_high
    queries = mm(normed, wqkv[:, 0:HW])
    sq_high, sq_low = split(queries * queries)
    per_head = jnp.where(iota((HW, HW), 0) // HEAD == iota((HW, HW), 1) // HEAD, 1.0 / HEAD, 0.0).astype(BF16)
    mean_sq = mm(sq_high, per_head) + mm(sq_low, per_head)
    queries = (queries * lax.rsqrt(mean_sq + EPSILON) * gain_ref[0:1, :]).astype(BF16).astype(F32)
    queries = queries * (gain_ref[1:2, :] * (HEAD ** (-0.5) * LOG2E))
    first_half = iota((TOK, 2 * HEAD), 1) < HEAD
    for two in range(HEADS // 2):
        columns = slice(two * 2 * HEAD, (two + 1) * 2 * HEAD)
        both = queries[:, columns]
        mine = jnp.concatenate([jnp.where(first_half, both, 0.0), jnp.where(first_half, 0.0, both)], axis=0)
        q_high, q_low = split(mine)
        k_high, k_low = keys_t_high[columns, :], keys_t_low[columns, :]
        umat[two * 256 : (two + 1) * 256, :] = (
            mm(q_high, k_high) + (mm(q_high, k_low) + mm(q_low, k_high))).astype(BF16)
    values_of = mm(scaled_high, wqkv[:, 2 * HW : 3 * HW]) + mm(scaled_low, wqkv[:, 2 * HW : 3 * HW])
    bv_high[...], bv_low[...] = split(values_of)
    acc[...] = jnp.zeros((HEADS * TOK, FEAT), F32)

    def one_group(step, carry):
        back = jnp.where(step % 2 == 0, (NZ - step // 2) % NZ, (step + 1) // 2)
        z_from = (z_me + NZ - back) % NZ
        parts = []
        for x_back in range(NX):
            source = ((x_me + NX - x_back) % NX) * NZ + z_from
            shift = (me + N_SEQ - source) % N_SEQ

            @pl.when((step > 0) | (x_back > 0))
            def _():
                pltpu.make_async_remote_copy(
                    src_ref=gath.at[source], dst_ref=gath.at[source], send_sem=gs_sem.at[shift],
                    recv_sem=gr_sem.at[shift], device_id={"seq": me}, device_id_type=mesh_ids).wait_recv()

        for x_back in range(NX):
            source = ((x_me + NX - x_back) % NX) * NZ + z_from
            parts.append(gath[source].astype(F32))
        rows = jnp.concatenate(parts, axis=1)
        std = rows[12:13, :] + rows[13:14, :]
        log_std = LOG2E * jnp.log(std)
        which = iota((8, GROUP), 0)
        std_rows = jnp.where(which == 0, rows[12:13, :], jnp.where(which == 1, rows[13:14, :], 0.0))
        ft_ref[...] = jnp.concatenate(
            one_hots(rows[8:11, :], GROUP) + [rows[0:8, :], std_rows, jnp.zeros((48, GROUP), F32)], axis=0).astype(BF16)
        keys = mm(bkt[...], ft_ref[...])
        scores = mm(umat[...], ft_ref[...])
        for head in range(HEADS):
            keys_h = keys[head * HEAD : (head + 1) * HEAD, :]
            mean_h = jnp.sum(keys_h * keys_h, axis=0, keepdims=True) * (1.0 / HEAD)
            inv = lax.rsqrt(mean_h + EPSILON * (std * std))
            p_ref[head * TOK : (head + 1) * TOK, :] = jnp.exp2(
                scores[head * TOK : (head + 1) * TOK, :] * inv - log_std).astype(BF16)
        acc[...] += mm_nt(p_ref[...], ft_ref[...])
        return carry

    lax.fori_loop(0, NZ, one_group, 0)

    loads[11].wait()
    lane = iota((TOK, FEAT), 1)
    pieces = []
    for two in range(HEADS // 2):
        columns = slice(two * 2 * HEAD, (two + 1) * 2 * HEAD)
        halves = []
        for odd in range(2):
            head = 2 * two + odd
            total = acc[head * TOK : (head + 1) * TOK, :]
            denom = jnp.sum(jnp.where((lane == 200) | (lane == 201), total, 0.0), axis=1, keepdims=True)
            halves.append(total * (1.0 / denom))
        t_high, t_low = split(jnp.concatenate(halves, axis=0))
        found = mm(t_high, bv_high[:, columns]) + (mm(t_low, bv_high[:, columns]) + mm(t_high, bv_low[:, columns]))
        pieces.append(jnp.where(first_half, found[0:TOK, :], found[TOK : 2 * TOK, :]))
    attended = jnp.concatenate(pieces, axis=1).astype(BF16)
    hidden = hid_ref[...] + mod_ref[2] * mm(attended, wout[...])
    center = hidden - jnp.mean(hidden, axis=1, keepdims=True)
    variance = jnp.mean(center * center, axis=1, keepdims=True)
    final = center * lax.rsqrt(variance + EPSILON) * (1.0 + mod_ref[4]) + mod_ref[3]
    vel_ref[...] = mm3(head_ref[...], final, mm_nt)
    swap = pltpu.make_async_remote_copy(
        src_ref=vel_ref, dst_ref=vel_in, send_sem=ps_sem, recv_sem=pr_sem,
        device_id={"pair": other}, device_id_type=mesh_ids)
    swap.start()

    own_rows = jnp.broadcast_to(own_ref[...], (TOK, TOK)).astype(F32)
    own_cols = own_rows.T
    earlier = (own_rows == own_cols) & (iota((TOK, TOK), 0) < iota((TOK, TOK), 1))
    rank = jnp.sum(jnp.where(earlier, 1.0, 0.0), axis=0, keepdims=True)
    ranked = rank == ((iota((TOK, TOK), 0) // LAT) % CAP).astype(F32)
    own96 = jnp.broadcast_to(own_ref[...], (3 * N_SEQ, TOK))
    owner = iota((3 * N_SEQ, TOK), 0)
    owner = jnp.where(owner < N_SEQ, owner, jnp.where(owner < 2 * N_SEQ, owner - N_SEQ - 1, owner - 2 * N_SEQ + 1))
    dispatch = jnp.where(own96 == owner, 1.0, 0.0).astype(BF16)
    swap.wait()
    mine, theirs = vel_ref[...], vel_in[...]
    is_cond = pair == 0
    cond = jnp.where(is_cond, mine, theirs)
    uncond = jnp.where(is_cond, theirs, mine)
    clean = lat_ref[...] - step_ref[0] * (uncond + GUIDANCE * (cond - uncond))
    wide = jnp.where(ranked, jnp.concatenate([clean] * (TOK // LAT), axis=0), 0.0)
    wide_high, wide_low = split(wide)
    packed = mm_nt(dispatch, wide_high) + mm_nt(dispatch, wide_low)
    sendbuf[:, 0, :] = jnp.where(
        iota((N_SEQ, TOK), 1) < LAT * CAP, packed[0:N_SEQ, :], packed[N_SEQ : 2 * N_SEQ, :])
    sendbuf[:, 1, :] = packed[2 * N_SEQ :, :]

    keep = pltpu.make_async_copy(sendbuf.at[me], rbuf.at[me], lsem.at[12])
    keep.start()
    for shift in range(1, N_SEQ):
        dest = (me + shift) % N_SEQ
        pltpu.make_async_remote_copy(
            src_ref=sendbuf.at[dest], dst_ref=rbuf.at[me], send_sem=as_sem.at[shift], recv_sem=ar_sem.at[shift],
            device_id={"seq": dest}, device_id_type=mesh_ids).start()

    lower = jnp.maximum(me - 1, 0)
    upper = jnp.minimum(me + 1, N_SEQ - 1)
    nb_ref[0:1, :] = gath[lower].astype(F32)[11:12, :]
    nb_ref[1:2, :] = gath[upper].astype(F32)[11:12, :]
    nb_ref[2:8, :] = jnp.zeros((6, TOK), F32)
    for shift in range(1, N_SEQ):
        g_copy(shift).wait_send()
    keep.wait()
    for shift in range(1, N_SEQ):
        source = (me + N_SEQ - shift) % N_SEQ
        pltpu.make_async_remote_copy(
            src_ref=sendbuf.at[source], dst_ref=rbuf.at[source], send_sem=as_sem.at[shift], recv_sem=ar_sem.at[shift],
            device_id={"seq": me}, device_id_type=mesh_ids).wait()
    x_ref[...] = rbuf[...]


TRIPLE = 3
PARTS = KOFF // TRIPLE


def conv_kernel(
    x_ref, nb_ref, km_hbm, dproj_hbm, wt_hbm, owned_ref, dec_ref, km_ref, dproj_ref, wt, feats, prod_a, prod_b, acc, lsem
):
    loads = [
        pltpu.make_async_copy(source, target, lsem.at[number])
        for number, (source, target) in enumerate(((dproj_hbm, dproj_ref), (km_hbm, km_ref), (wt_hbm, wt)))
    ]
    for load in loads:
        load.start()
    x0 = x_ref[:, 0, :]
    x1 = x_ref[:, 1, :]

    pick = jnp.where(iota((N_SEQ, SLOTS), 1) // CAP == iota((N_SEQ, SLOTS), 0), 1.0, 0.0).astype(BF16)
    x0_high, x0_low = split(x0.T)
    x1_high, x1_low = split(x1)
    spread = mm(x0_high, pick) + mm(x0_low, pick)
    spread = jnp.where(iota((TOK, SLOTS), 1) % CAP == iota((TOK, SLOTS), 0) // LAT, spread, 0.0)
    owned = spread[0:LAT, :]
    for rank in range(1, CAP):
        owned = owned + spread[rank * LAT : (rank + 1) * LAT, :]
    owned_ref[...] = owned

    lane = iota((SLOTS, TOK), 1)
    own_rows = jnp.where(lane // LAT == iota((SLOTS, TOK), 0) // N_SEQ, jnp.concatenate([x0] * CAP, axis=0), 0.0)
    sub = iota((HALO, TOK), 0)
    lane = iota((HALO, TOK), 1)
    parts = [own_rows]
    x0_high, x0_low = split(x0)
    for side, halves in ((0, (x0_high, x0_low)), (1, (x1_high, x1_low))):
        blocks = jnp.broadcast_to(nb_ref[side : side + 1, :], (HALO, TOK))
        first = 8 if side == 0 else 0
        chosen = jnp.sum(jnp.where(lane == sub // BLK + first, blocks, 0.0), axis=1, keepdims=True)
        source = chosen * (BLK // CAP) + ((iota((HALO, 1), 0) % BLK) // CAP).astype(F32)
        pick = jnp.where(iota((HALO, N_SEQ), 1).astype(F32) == source, 1.0, 0.0).astype(BF16)
        rows = mm(pick, halves[0]) + mm(pick, halves[1])
        offset = CAP if side == 0 else 0
        parts.append(jnp.where(lane // LAT == sub % CAP + offset, rows, 0.0))
    latents = jnp.concatenate(parts, axis=0)
    loads[0].wait()
    proj = jnp.concatenate([dproj_ref[...]] * (TOK // LAT), axis=0).T
    value = mm3(proj, latents, mm_nt)
    feats[...] = (value / (1.0 + jnp.exp(-value))).astype(BF16)
    acc[...] = jnp.zeros((OUT_DEV, FINE), F32)
    loads[1].wait()
    loads[2].wait()

    def products(part, target):
        for i in range(TRIPLE):
            target[i] = mm(wt[part * TRIPLE + i], feats[...])

    def gather(part, source):
        for i in range(TRIPLE):
            index = km_ref[part * TRIPLE + i]
            index = jnp.where(index < SLOTS, (index % CAP) * N_SEQ + index // CAP, index)
            for block in range(FINE // TOK):
                columns = slice(block * TOK, (block + 1) * TOK)
                here = index[:, columns]
                spot = jnp.broadcast_to(here % TOK, (OUT_DEV, TOK))
                chunk = jnp.broadcast_to(here // TOK, (OUT_DEV, TOK))
                value = jnp.zeros((OUT_DEV, TOK), F32)
                for c in range(4):
                    found = jnp.take_along_axis(
                        source[i, :, c * TOK : (c + 1) * TOK], spot, axis=1, mode="promise_in_bounds")
                    value = jnp.where(chunk == c, found, value)
                acc[:, columns] += value

    products(0, prod_a)

    def two_parts(i, carry):
        products(2 * i + 1, prod_b)
        gather(2 * i, prod_a)
        products(2 * i + 2, prod_a)
        gather(2 * i + 1, prod_b)
        return carry

    lax.fori_loop(0, PARTS // 2, two_parts, 0)
    gather(PARTS - 1, prod_a)
    dec_ref[...] = acc[...].astype(BF16)


def vmem(count):
    return [pl.BlockSpec(memory_space=pltpu.VMEM)] * count


def hbm(count):
    return [pl.BlockSpec(memory_space=pltpu.HBM)] * count


def per_device(
    latents, voxel_coords, owner_map, step_time, modulation, in_proj, qkv_proj, norm_gain, out_proj, head_proj,
    decoder_projection, border_blocks, kernel_map, conv_weight,
):
    table = centred_position_table()
    table_high = table.astype(jnp.bfloat16)
    table_low = (table - table_high.astype(np.float32)).astype(jnp.bfloat16)
    dma = pltpu.SemaphoreType.DMA
    gathered, borders = pl.pallas_call(
        flow_kernel,
        out_shape=(jax.ShapeDtypeStruct((N_SEQ, 2, TOK), F32), jax.ShapeDtypeStruct((8, TOK), F32)),
        in_specs=hbm(3) + [pl.BlockSpec(memory_space=pltpu.SMEM)] + hbm(9),
        out_specs=tuple(vmem(2)),
        scratch_shapes=[
            pltpu.VMEM((LAT, TOK), F32),
            pltpu.VMEM((3, 1, TOK), jnp.int32),
            pltpu.VMEM((1, TOK), jnp.int32),
            pltpu.VMEM((5, 1, D), F32),
            pltpu.VMEM((LAT, D), F32),
            pltpu.VMEM((2, HW), F32),
            pltpu.VMEM((LAT, D), F32),
            pltpu.VMEM((2, 8), jnp.int32),
            pltpu.VMEM((3 * RES, D), BF16),
            pltpu.VMEM((3 * RES, D), BF16),
            pltpu.VMEM((D, 3 * HW), BF16),
            pltpu.VMEM((HW, D), BF16),
            pltpu.VMEM((N_SEQ, 16, TOK), BF16),
            pltpu.VMEM((16, TOK), F32),
            pltpu.VMEM((HW, FEAT), BF16),
            pltpu.VMEM((FEAT, HW), BF16),
            pltpu.VMEM((FEAT, HW), BF16),
            pltpu.VMEM((HEADS * TOK, FEAT), BF16),
            pltpu.VMEM((TOK, D), F32),
            pltpu.VMEM((FEAT, GROUP), BF16),
            pltpu.VMEM((HEADS * TOK, GROUP), BF16),
            pltpu.VMEM((HEADS * TOK, FEAT), F32),
            pltpu.VMEM((LAT, TOK), F32),
            pltpu.VMEM((LAT, TOK), F32),
            pltpu.VMEM((N_SEQ, 2, TOK), F32),
            pltpu.VMEM((N_SEQ, 2, TOK), F32),
            dma((13,)), dma((N_SEQ,)), dma((N_SEQ,)), dma, dma, dma((N_SEQ,)), dma((N_SEQ,)),
        ],
        compiler_params=pltpu.CompilerParams(collective_id=0, has_side_effects=True, vmem_limit_bytes=67043328),
        name="flow",
    )(
        latents[0], jnp.transpose(voxel_coords, (1, 0, 2)), owner_map.reshape(1, TOK), step_time,
        modulation.reshape(5, 1, D), in_proj, norm_gain, head_proj.T, border_blocks[0, 0], jnp.asarray(table_high),
        jnp.asarray(table_low), qkv_proj, out_proj,
    )
    owned, decoded = pl.pallas_call(
        conv_kernel,
        out_shape=(jax.ShapeDtypeStruct((LAT, SLOTS), F32), jax.ShapeDtypeStruct((OUT_DEV, FINE), BF16)),
        in_specs=vmem(2) + hbm(3),
        out_specs=tuple(vmem(2)),
        scratch_shapes=[
            pltpu.VMEM((KOFF, 1, FINE), jnp.int32),
            pltpu.VMEM((LAT, DEC), F32),
            pltpu.VMEM((KOFF, OUT_DEV, DEC), BF16),
            pltpu.VMEM((DEC, 2 * SLOTS), BF16),
            pltpu.VMEM((TRIPLE, OUT_DEV, 2 * SLOTS), F32),
            pltpu.VMEM((TRIPLE, OUT_DEV, 2 * SLOTS), F32),
            pltpu.VMEM((OUT_DEV, FINE), F32),
            dma((3,)),
        ],
        compiler_params=pltpu.CompilerParams(vmem_limit_bytes=67043328),
        name="conv",
    )(gathered, borders, kernel_map.reshape(KOFF, 1, FINE), decoder_projection, jnp.swapaxes(conv_weight, 1, 2))
    return owned[None, None], decoded.T[None, None]


def solution(mesh):
    placed = (
        P("asset", None, "seq"),
        P("asset", None, "seq"),
        P("asset", "seq", None),
        P("asset"),
        P("asset", "pair", None, None),
        P(),
        P(),
        P(),
        P(),
        P(),
        P(),
        P("asset", "seq", None, None),
        P("asset", "seq", None, None),
        P(None, None, "pair"),
    )
    return jax.shard_map(
        per_device,
        mesh=mesh,
        in_specs=placed,
        out_specs=(P("asset", "seq", None, None), P("asset", "seq", None, "pair")),
        check_vma=False,
    )
```

time: 94.5 us -> 51.7 us (0.55)
  Pallas kernels: 71.6 us -> 50.2 us
  local copies, waits for them, and re-layouts: 20.9 us -> 0 us
    unnamed x26 -> x0, local copies, waits for them, and re-layouts: 20.9 us -> none
    pallas_call x1, Pallas kernels: 31.6 us -> 16.6 us  [per_device(): pl.pallas_call(conv_kernel, out_shape=(jax.ShapeDtypeStruct((LAT, SLOTS),...]
    pallas_call x1, Pallas kernels: 40 us -> 33.6 us  [per_device(): pl.pallas_call(flow_kernel, out_shape=(jax.ShapeDtypeStruct((N_SEQ, 2, TO...]
where the time goes in v2:
time: 51.7 us; the launch traced here: 51.5 us
  Pallas kernels  50.2 us (97%)
  between operations  1.29 us (2%)
    pallas_call x1, Pallas kernels, per_device(): pl.pallas_call(flow_kernel, out_shape=(jax.ShapeDtypeStruct((N_SEQ, 2, TO...  33.6 us
    pallas_call x1, Pallas kernels, per_device(): pl.pallas_call(conv_kernel, out_shape=(jax.ShapeDtypeStruct((LAT, SLOTS),...  16.6 us

profile of v2, /device:TPU:1, one launch (start us, length us, event | category | flops | bytes accessed | tf_op | source)
XLA Modules:
  0.0 51.5 jit_solution(17394244390050191628)
XLA Ops:
  1.3 33.6 %flow.1 = (f32[32,2,128]{2,1,0:T(2,128)}, f32[8,128]{1,0:T(8,128)}) custom-call(f32[8,128]{1,0:T(8,128)} %bitcast.16, s32[3,1,128]{2,1,0:T(1,128)} %bitcast.17, s32[1,128]{1,0:T(1,128)} %bitcast.19, f32[1]{0:T(128)S(6)} %copy.18.step_ref, f32[5,1,1024]{2,1,0:T(1,128)} %bitcast.15, f32[8,1024]{1,0:T(8,128)} %inp_hbm.1, f32[2,512]{1,0:T(2,128)} %gain_hbm.1, ...), custom_call_target="tpu_custom_call" | custom-call | tf_op jit(solution)/shard_map/flow/pallas_call | solution.py:389
  34.9 16.6 %conv.1 = (f32[8,256]{1,0:T(8,128)}, bf16[96,1024]{1,0:T(8,128)(2,1)}) custom-call(f32[32,2,128]{2,1,0:T(2,128)} %get-tuple-element.6.x_ref, f32[8,128]{1,0:T(8,128)} %get-tuple-element.7.nb_ref, s32[27,1,1024]{2,1,0:T(1,128)} %bitcast.13, f32[8,768]{1,0:T(8,128)} %dproj_hbm.1, bf16[27,96,768]{2,1,0:T(8,128)(2,1)} %bitcast.12), custom_call_target="tpu_custom_call" | custom-call | tf_op jit(solution)/shard_map/conv/pallas_call | solution.py:430

commit v3 on v2

--- a/solution.py
+++ b/solution.py
@@ -288,10 +288,13 @@
 
 TRIPLE = 3
 PARTS = KOFF // TRIPLE
+BLOCKS = FINE // TOK
+SHARED = 0
 
 
 def conv_kernel(
-    x_ref, nb_ref, km_hbm, dproj_hbm, wt_hbm, owned_ref, dec_ref, km_ref, dproj_ref, wt, feats, prod_a, prod_b, acc, lsem
+    x_ref, nb_ref, km_hbm, dproj_hbm, wt_hbm, owned_ref, dec_ref, km_ref, dproj_ref, wt, feats, spot_ref, chunk_ref,
+    near_ref, far_ref, prod_a, prod_b, acc_x, acc_m, lsem
 ):
     loads = [
         pltpu.make_async_copy(source, target, lsem.at[number])
@@ -303,9 +306,8 @@
     x1 = x_ref[:, 1, :]
 
     pick = jnp.where(iota((N_SEQ, SLOTS), 1) // CAP == iota((N_SEQ, SLOTS), 0), 1.0, 0.0).astype(BF16)
-    x0_high, x0_low = split(x0.T)
-    x1_high, x1_low = split(x1)
-    spread = mm(x0_high, pick) + mm(x0_low, pick)
+    xt_high, xt_low = split(x0.T)
+    spread = mm(xt_high, pick) + mm(xt_low, pick)
     spread = jnp.where(iota((TOK, SLOTS), 1) % CAP == iota((TOK, SLOTS), 0) // LAT, spread, 0.0)
     owned = spread[0:LAT, :]
     for rank in range(1, CAP):
@@ -317,57 +319,90 @@
     sub = iota((HALO, TOK), 0)
     lane = iota((HALO, TOK), 1)
     parts = [own_rows]
-    x0_high, x0_low = split(x0)
-    for side, halves in ((0, (x0_high, x0_low)), (1, (x1_high, x1_low))):
+    for side, x_side in ((0, x0), (1, x1)):
         blocks = jnp.broadcast_to(nb_ref[side : side + 1, :], (HALO, TOK))
         first = 8 if side == 0 else 0
         chosen = jnp.sum(jnp.where(lane == sub // BLK + first, blocks, 0.0), axis=1, keepdims=True)
         source = chosen * (BLK // CAP) + ((iota((HALO, 1), 0) % BLK) // CAP).astype(F32)
         pick = jnp.where(iota((HALO, N_SEQ), 1).astype(F32) == source, 1.0, 0.0).astype(BF16)
-        rows = mm(pick, halves[0]) + mm(pick, halves[1])
+        x_high, x_low = split(x_side)
+        rows = mm(pick, x_high) + mm(pick, x_low)
         offset = CAP if side == 0 else 0
         parts.append(jnp.where(lane // LAT == sub % CAP + offset, rows, 0.0))
-    latents = jnp.concatenate(parts, axis=0)
+    l_high, l_low = split(jnp.concatenate(parts, axis=0))
     loads[0].wait()
-    proj = jnp.concatenate([dproj_ref[...]] * (TOK // LAT), axis=0).T
-    value = mm3(proj, latents, mm_nt)
-    feats[...] = (value / (1.0 + jnp.exp(-value))).astype(BF16)
-    acc[...] = jnp.zeros((OUT_DEV, FINE), F32)
+    p_high, p_low = split(dproj_ref[...])
+    p_high = jnp.concatenate([p_high.astype(F32)] * (TOK // LAT), axis=0).astype(BF16)
+    p_low = jnp.concatenate([p_low.astype(F32)] * (TOK // LAT), axis=0).astype(BF16)
+    value = mm(jnp.concatenate([l_high, l_low], axis=1), jnp.concatenate([p_high, p_high], axis=0)) + mm(l_high, p_low)
+    half = value * 0.5
+    feats[...] = (half * jnp.tanh(half) + half).astype(BF16)
+    acc_x[...] = jnp.zeros((OUT_DEV, FINE), F32)
+    acc_m[...] = jnp.zeros((OUT_DEV, FINE), F32)
     loads[1].wait()
+    index = km_ref[...]
+    index = jnp.where(index < SLOTS, ((index & (CAP - 1)) << 5) + (index >> 3), index)
+    spot_ref[...] = index & (TOK - 1)
+    chunk_ref[...] = index >> 7
+    near_ref[...] = jnp.minimum(index, 300).astype(F32)
+    far_ref[...] = jnp.where(index >= SLOTS, jnp.minimum(index - SLOTS, 300), 300).astype(F32)
     loads[2].wait()
 
-    def products(part, target):
-        for i in range(TRIPLE):
-            target[i] = mm(wt[part * TRIPLE + i], feats[...])
-
-    def gather(part, source):
-        for i in range(TRIPLE):
-            index = km_ref[part * TRIPLE + i]
-            index = jnp.where(index < SLOTS, (index % CAP) * N_SEQ + index // CAP, index)
-            for block in range(FINE // TOK):
-                columns = slice(block * TOK, (block + 1) * TOK)
-                here = index[:, columns]
-                spot = jnp.broadcast_to(here % TOK, (OUT_DEV, TOK))
-                chunk = jnp.broadcast_to(here // TOK, (OUT_DEV, TOK))
-                value = jnp.zeros((OUT_DEV, TOK), F32)
-                for c in range(4):
-                    found = jnp.take_along_axis(
-                        source[i, :, c * TOK : (c + 1) * TOK], spot, axis=1, mode="promise_in_bounds")
-                    value = jnp.where(chunk == c, found, value)
-                acc[:, columns] += value
-
-    products(0, prod_a)
+    def product(part, half, target):
+        rows = pl.ds(pl.multiple_of(part * (TRIPLE * OUT_DEV), TRIPLE * OUT_DEV), TRIPLE * OUT_DEV)
+        table = slice(half * SLOTS, (half + 1) * SLOTS)
+        target[:, table] = mm_nt(wt[rows, :], feats[table, :])
+
+    def by_gather(number, source, block):
+        columns = slice(block * TOK, (block + 1) * TOK)
+        spot = jnp.broadcast_to(spot_ref[number, block : block + 1, :], (OUT_DEV, TOK))
+        chunk = jnp.broadcast_to(chunk_ref[number, block : block + 1, :], (OUT_DEV, TOK))
+        value = jnp.zeros((OUT_DEV, TOK), F32)
+        for c in range(4):
+            found = jnp.take_along_axis(source[:, c * TOK : (c + 1) * TOK], spot, axis=1, mode="promise_in_bounds")
+            value = jnp.where(chunk == c, found, value)
+        acc_x[:, columns] += value
+
+    first_ids = iota((16, TOK), 0).astype(F32).astype(BF16)
+
+    def hot_rows(number, blocks):
+        columns = []
+        for block in blocks:
+            rows = []
+            for which in (near_ref, far_ref):
+                row = jnp.broadcast_to(which[number, block : block + 1, :], (16, TOK)).astype(BF16) - first_ids
+                for j in range(SLOTS // 16):
+                    rows.append(jnp.where(row == jnp.bfloat16(16 * j), jnp.bfloat16(1), jnp.bfloat16(0)))
+            columns.append(jnp.concatenate(rows, axis=0))
+        return jnp.concatenate(columns, axis=1)
+
+    def pick_rows(part, source, target):
+        first = part * TRIPLE
+        for quarter in range(4):
+            blocks = (2 * quarter, 2 * quarter + 1)
+            columns = slice(quarter * 2 * TOK, (quarter + 1) * 2 * TOK)
+            if target is not None and quarter % 2 == 0:
+                product(part + 1, quarter // 2, target)
+            found = mm(source[2 * OUT_DEV :, :].astype(BF16), hot_rows(first + 2, blocks))
+            if quarter >= SHARED:
+                found += mm(source[OUT_DEV : 2 * OUT_DEV, :].astype(BF16), hot_rows(first + 1, blocks))
+            acc_m[:, columns] += found
+            for block in blocks:
+                by_gather(first, source.at[0:OUT_DEV], block)
+                if quarter < SHARED:
+                    by_gather(first + 1, source.at[OUT_DEV : 2 * OUT_DEV], block)
+
+    for half in range(2):
+        product(0, half, prod_a)
 
     def two_parts(i, carry):
-        products(2 * i + 1, prod_b)
-        gather(2 * i, prod_a)
-        products(2 * i + 2, prod_a)
-        gather(2 * i + 1, prod_b)
+        pick_rows(2 * i, prod_a, prod_b)
+        pick_rows(2 * i + 1, prod_b, prod_a)
         return carry
 
     lax.fori_loop(0, PARTS // 2, two_parts, 0)
-    gather(PARTS - 1, prod_a)
-    dec_ref[...] = acc[...].astype(BF16)
+    pick_rows(PARTS - 1, prod_a, None)
+    dec_ref[...] = (acc_x[...] + acc_m[...]).astype(BF16)
 
 
 def vmem(count):
@@ -433,18 +468,23 @@
         in_specs=vmem(2) + hbm(3),
         out_specs=tuple(vmem(2)),
         scratch_shapes=[
-            pltpu.VMEM((KOFF, 1, FINE), jnp.int32),
+            pltpu.VMEM((KOFF, BLOCKS, TOK), jnp.int32),
             pltpu.VMEM((LAT, DEC), F32),
-            pltpu.VMEM((KOFF, OUT_DEV, DEC), BF16),
-            pltpu.VMEM((DEC, 2 * SLOTS), BF16),
-            pltpu.VMEM((TRIPLE, OUT_DEV, 2 * SLOTS), F32),
-            pltpu.VMEM((TRIPLE, OUT_DEV, 2 * SLOTS), F32),
+            pltpu.VMEM((KOFF * OUT_DEV, DEC), BF16),
+            pltpu.VMEM((2 * SLOTS, DEC), BF16),
+            pltpu.VMEM((KOFF, BLOCKS, TOK), jnp.int32),
+            pltpu.VMEM((KOFF, BLOCKS, TOK), jnp.int32),
+            pltpu.VMEM((KOFF, BLOCKS, TOK), F32),
+            pltpu.VMEM((KOFF, BLOCKS, TOK), F32),
+            pltpu.VMEM((TRIPLE * OUT_DEV, 2 * SLOTS), F32),
+            pltpu.VMEM((TRIPLE * OUT_DEV, 2 * SLOTS), F32),
+            pltpu.VMEM((OUT_DEV, FINE), F32),
             pltpu.VMEM((OUT_DEV, FINE), F32),
             dma((3,)),
         ],
         compiler_params=pltpu.CompilerParams(vmem_limit_bytes=67043328),
         name="conv",
-    )(gathered, borders, kernel_map.reshape(KOFF, 1, FINE), decoder_projection, jnp.swapaxes(conv_weight, 1, 2))
+    )(gathered, borders, kernel_map.reshape(KOFF, BLOCKS, TOK), decoder_projection, jnp.swapaxes(conv_weight, 1, 2).reshape(KOFF * OUT_DEV, DEC))
     return owned[None, None], decoded.T[None, None]
 
 

time: 51.7 us -> 45.4 us (0.88)
  Pallas kernels: 50.2 us -> 43.9 us
    pallas_call x1, Pallas kernels: 16.6 us -> 10.3 us  [per_device(): pl.pallas_call(conv_kernel, out_shape=(jax.ShapeDtypeStruct((LAT, SLOTS),...]
where the time goes in v3:
time: 45.4 us; the launch traced here: 45.2 us
  Pallas kernels  43.9 us (97%)
  between operations  1.29 us (3%)
    pallas_call x1, Pallas kernels, per_device(): pl.pallas_call(flow_kernel, out_shape=(jax.ShapeDtypeStruct((N_SEQ, 2, TO...  33.6 us
    pallas_call x1, Pallas kernels, per_device(): pl.pallas_call(conv_kernel, out_shape=(jax.ShapeDtypeStruct((LAT, SLOTS),...  10.3 us

profile of v3, /device:TPU:1, one launch (start us, length us, event | category | flops | bytes accessed | tf_op | source)
XLA Modules:
  0.0 45.2 jit_solution(6707757007505472831)
XLA Ops:
  1.3 33.6 %flow.1 = (f32[32,2,128]{2,1,0:T(2,128)}, f32[8,128]{1,0:T(8,128)}) custom-call(f32[8,128]{1,0:T(8,128)} %bitcast.18, s32[3,1,128]{2,1,0:T(1,128)} %bitcast.19, s32[1,128]{1,0:T(1,128)} %bitcast.21, f32[1]{0:T(128)S(6)} %copy.18.step_ref, f32[5,1,1024]{2,1,0:T(1,128)} %bitcast.17, f32[8,1024]{1,0:T(8,128)} %inp_hbm.1, f32[2,512]{1,0:T(2,128)} %gain_hbm.1, ...), custom_call_target="tpu_custom_call" | custom-call | tf_op jit(solution)/shard_map/flow/pallas_call | solution.py:424
  34.9 10.3 %conv.1 = (f32[8,256]{1,0:T(8,128)}, bf16[96,1024]{1,0:T(8,128)(2,1)}) custom-call(f32[32,2,128]{2,1,0:T(2,128)} %get-tuple-element.6.x_ref, f32[8,128]{1,0:T(8,128)} %get-tuple-element.7.nb_ref, s32[27,8,128]{2,1,0:T(8,128)} %bitcast.15, f32[8,768]{1,0:T(8,128)} %dproj_hbm.1, bf16[2592,768]{1,0:T(8,128)(2,1)} %bitcast.14), custom_call_target="tpu_custom_call" | custom-call | tf_op jit(solution)/shard_map/conv/pallas_call | solution.py:465

commit v4 on v3

--- a/solution.py
+++ b/solution.py
@@ -31,7 +31,6 @@
 EPSILON = 1e-06
 GUIDANCE = 3.0
 LOG2E = 1.4426950408889634
-HI = lax.Precision.HIGHEST
 F32 = jnp.float32
 BF16 = jnp.bfloat16
 
@@ -60,16 +59,6 @@
     return lax.dot_general(a, b, (((1,), (1,)), ((), ())), preferred_element_type=F32)
 
 
-def mm3(a, b, product=mm):
-    a_high, a_low = split(a)
-    b_high, b_low = split(b)
-    return product(a_high, b_high) + (product(a_high, b_low) + product(a_low, b_high))
-
-
-def exact(a, b):
-    return jnp.dot(a, b, precision=HI, preferred_element_type=F32)
-
-
 def iota(shape, dim):
     return lax.broadcasted_iota(jnp.int32, shape, dim)
 
@@ -81,10 +70,11 @@
 
 def flow_kernel(
     lat_hbm, coord_hbm, own_hbm, step_ref, mod_hbm, inp_hbm, gain_hbm, head_hbm, bb_hbm, tabh_hbm, tabl_hbm, wqkv_hbm,
-    wout_hbm,
-    x_ref, nb_ref,
-    lat_ref, coord_ref, own_ref, mod_ref, inp_ref, gain_ref, head_ref, bb_ref, tabh, tabl, wqkv, wout,
-    gath, stage, bkt, bv_high, bv_low, umat, hid_ref, ft_ref, p_ref, acc, vel_ref, vel_in, sendbuf, rbuf,
+    wout_hbm, wt_hbm, km_hbm,
+    x_ref, nb_ref, wt_ref, spot_ref, chunk_ref, near_ref, far_ref,
+    lat_ref, coord_ref, own_ref, mod_ref, inp_ref, gain_ref, head_ref, bb_ref, tabh, tabl, wqkv, wout, km_ref,
+    gath, stage, scaled, bkt, bv, umat, hid_ref, ft_ref, fs_ref, p_ref, acc, hp_high, hp_low, hp_const, vel_ref, vel_in,
+    sendbuf, rbuf,
     lsem, gs_sem, gr_sem, ps_sem, pr_sem, as_sem, ar_sem,
 ):
     me = lax.axis_index("seq")
@@ -94,20 +84,20 @@
     z_me = me % NZ
     mesh_ids = pl.DeviceIdType.MESH
 
-    barrier = pltpu.get_barrier_semaphore()
-    for shift in range(1, N_SEQ):
-        pl.semaphore_signal(barrier, inc=1, device_id={"seq": (me + shift) % N_SEQ}, device_id_type=mesh_ids)
-    pl.semaphore_signal(barrier, inc=1, device_id={"pair": other}, device_id_type=mesh_ids)
-
     loads = [
         pltpu.make_async_copy(source, target, lsem.at[number])
         for number, (source, target) in enumerate((
             (lat_hbm, lat_ref), (coord_hbm, coord_ref), (own_hbm, own_ref), (mod_hbm, mod_ref), (inp_hbm, inp_ref),
             (gain_hbm, gain_ref), (head_hbm, head_ref), (bb_hbm, bb_ref), (tabh_hbm, tabh), (tabl_hbm, tabl),
-            (wqkv_hbm, wqkv), (wout_hbm, wout)))
+            (wqkv_hbm, wqkv), (wout_hbm, wout), (km_hbm, km_ref), (wt_hbm, wt_ref)))
     ]
-    for load in loads:
+    for load in loads[:12]:
         load.start()
+
+    barrier = pltpu.get_barrier_semaphore()
+    for shift in range(1, N_SEQ):
+        pl.semaphore_signal(barrier, inc=1, device_id={"seq": (me + shift) % N_SEQ}, device_id_type=mesh_ids)
+    pl.semaphore_signal(barrier, inc=1, device_id={"pair": other}, device_id_type=mesh_ids)
     for load in loads[:10]:
         load.wait()
 
@@ -150,70 +140,79 @@
 
     scale1 = 1.0 + mod_ref[1]
     normed = (center * lax.rsqrt(variance + EPSILON) * scale1 + mod_ref[0]).astype(BF16)
+    for axis in range(3):
+        rows = slice(axis * RES, (axis + 1) * RES)
+        scaled[rows, :] = ((tabh[rows, :].astype(F32) + tabl[rows, :].astype(F32)) * scale1).astype(BF16)
     shift_rows = jnp.where(iota((8, D), 0) < 2, jnp.broadcast_to(mod_ref[0], (8, D)), 0.0)
-    scaled = jnp.concatenate(
-        [(tabh[...].astype(F32) + tabl[...].astype(F32)) * scale1, inp * scale1, shift_rows, jnp.zeros((48, D), F32)],
-        axis=0)
-    scaled_high, scaled_low = split(scaled)
+    scaled[3 * RES :, :] = jnp.concatenate([inp * scale1, shift_rows, jnp.zeros((48, D), F32)], axis=0).astype(BF16)
     loads[10].wait()
-    keys_of = mm(scaled_high, wqkv[:, HW : 2 * HW]) + mm(scaled_low, wqkv[:, HW : 2 * HW])
-    keys_t_high, keys_t_low = split(keys_of.T)
-    bkt[...] = keys_t_high
     queries = mm(normed, wqkv[:, 0:HW])
-    sq_high, sq_low = split(queries * queries)
     per_head = jnp.where(iota((HW, HW), 0) // HEAD == iota((HW, HW), 1) // HEAD, 1.0 / HEAD, 0.0).astype(BF16)
-    mean_sq = mm(sq_high, per_head) + mm(sq_low, per_head)
-    queries = (queries * lax.rsqrt(mean_sq + EPSILON) * gain_ref[0:1, :]).astype(BF16).astype(F32)
-    queries = queries * (gain_ref[1:2, :] * (HEAD ** (-0.5) * LOG2E))
+    mean_sq = mm((queries * queries).astype(BF16), per_head)
+    queries = queries * lax.rsqrt(mean_sq + EPSILON) * (
+        gain_ref[0:1, :] * gain_ref[1:2, :] * (HEAD ** (-0.5) * LOG2E))
+    bkt[...] = mm(scaled[...], wqkv[:, HW : 2 * HW]).T.astype(BF16)
     first_half = iota((TOK, 2 * HEAD), 1) < HEAD
     for two in range(HEADS // 2):
         columns = slice(two * 2 * HEAD, (two + 1) * 2 * HEAD)
         both = queries[:, columns]
         mine = jnp.concatenate([jnp.where(first_half, both, 0.0), jnp.where(first_half, 0.0, both)], axis=0)
-        q_high, q_low = split(mine)
-        k_high, k_low = keys_t_high[columns, :], keys_t_low[columns, :]
-        umat[two * 256 : (two + 1) * 256, :] = (
-            mm(q_high, k_high) + (mm(q_high, k_low) + mm(q_low, k_high))).astype(BF16)
-    values_of = mm(scaled_high, wqkv[:, 2 * HW : 3 * HW]) + mm(scaled_low, wqkv[:, 2 * HW : 3 * HW])
-    bv_high[...], bv_low[...] = split(values_of)
+        umat[two * 256 : (two + 1) * 256, :] = mm(mine.astype(BF16), bkt[columns, :]).astype(BF16)
+    bv[...] = mm(scaled[...], wqkv[:, 2 * HW : 3 * HW]).astype(BF16)
+    head_scaled = head_ref[...] * (1.0 + mod_ref[4])
+    hp_high[...], hp_low[...] = split(head_scaled)
+    hp_const[...] = jnp.broadcast_to(jnp.sum(head_ref[...] * mod_ref[3], axis=1, keepdims=True), (LAT, TOK))
     acc[...] = jnp.zeros((HEADS * TOK, FEAT), F32)
-
-    def one_group(step, carry):
-        back = jnp.where(step % 2 == 0, (NZ - step // 2) % NZ, (step + 1) // 2)
-        z_from = (z_me + NZ - back) % NZ
-        parts = []
+    loads[12].start()
+    loads[13].start()
+
+    def arrived(z_back, first):
+        sources = []
+        z_from = (z_me + NZ - z_back) % NZ
         for x_back in range(NX):
             source = ((x_me + NX - x_back) % NX) * NZ + z_from
             shift = (me + N_SEQ - source) % N_SEQ
-
-            @pl.when((step > 0) | (x_back > 0))
-            def _():
+            sources.append(source)
+
+            def wait():
                 pltpu.make_async_remote_copy(
                     src_ref=gath.at[source], dst_ref=gath.at[source], send_sem=gs_sem.at[shift],
                     recv_sem=gr_sem.at[shift], device_id={"seq": me}, device_id_type=mesh_ids).wait_recv()
 
-        for x_back in range(NX):
-            source = ((x_me + NX - x_back) % NX) * NZ + z_from
-            parts.append(gath[source].astype(F32))
-        rows = jnp.concatenate(parts, axis=1)
-        std = rows[12:13, :] + rows[13:14, :]
-        log_std = LOG2E * jnp.log(std)
-        which = iota((8, GROUP), 0)
-        std_rows = jnp.where(which == 0, rows[12:13, :], jnp.where(which == 1, rows[13:14, :], 0.0))
-        ft_ref[...] = jnp.concatenate(
-            one_hots(rows[8:11, :], GROUP) + [rows[0:8, :], std_rows, jnp.zeros((48, GROUP), F32)], axis=0).astype(BF16)
+            if x_back == 0 and first is not None:
+                pl.when(first)(wait)
+            else:
+                wait()
+        return sources
+
+    def one_group(step, carry):
+        sources = arrived((NZ - step) % NZ, step > 0) + arrived(step + 1, None)
+        rows = jnp.concatenate([gath[source].astype(F32) for source in sources], axis=1)
+        std_high, std_low = rows[12:13, :], rows[13:14, :]
+        std = std_high + std_low
+        inv_std = 1.0 / std
+        which = iota((8, 2 * GROUP), 0)
+        ids = iota((RES, 2 * GROUP), 0).astype(F32)
+        for c in range(3):
+            hit = ids == rows[8 + c : 9 + c, :]
+            ft_ref[c * RES : (c + 1) * RES, :] = jnp.where(hit, 1.0, 0.0).astype(BF16)
+            fs_ref[c * RES : (c + 1) * RES, :] = jnp.where(hit, inv_std, 0.0).astype(BF16)
+        std_rows = jnp.where(which == 0, std_high, jnp.where(which == 1, std_low, 0.0))
+        pad = jnp.zeros((48, 2 * GROUP), F32)
+        ft_ref[3 * RES :, :] = jnp.concatenate([rows[0:8, :], std_rows, pad], axis=0).astype(BF16)
+        fs_ref[3 * RES :, :] = jnp.concatenate(
+            [rows[0:8, :] * inv_std, jnp.where(which == 0, 1.0, 0.0), pad], axis=0).astype(BF16)
         keys = mm(bkt[...], ft_ref[...])
         scores = mm(umat[...], ft_ref[...])
         for head in range(HEADS):
             keys_h = keys[head * HEAD : (head + 1) * HEAD, :]
             mean_h = jnp.sum(keys_h * keys_h, axis=0, keepdims=True) * (1.0 / HEAD)
             inv = lax.rsqrt(mean_h + EPSILON * (std * std))
-            p_ref[head * TOK : (head + 1) * TOK, :] = jnp.exp2(
-                scores[head * TOK : (head + 1) * TOK, :] * inv - log_std).astype(BF16)
-        acc[...] += mm_nt(p_ref[...], ft_ref[...])
+            p_ref[head * TOK : (head + 1) * TOK, :] = jnp.exp2(scores[head * TOK : (head + 1) * TOK, :] * inv).astype(BF16)
+        acc[...] += mm_nt(p_ref[...], fs_ref[...])
         return carry
 
-    lax.fori_loop(0, NZ, one_group, 0)
+    lax.fori_loop(0, NZ // 2, one_group, 0)
 
     loads[11].wait()
     lane = iota((TOK, FEAT), 1)
@@ -224,17 +223,30 @@
         for odd in range(2):
             head = 2 * two + odd
             total = acc[head * TOK : (head + 1) * TOK, :]
-            denom = jnp.sum(jnp.where((lane == 200) | (lane == 201), total, 0.0), axis=1, keepdims=True)
-            halves.append(total * (1.0 / denom))
-        t_high, t_low = split(jnp.concatenate(halves, axis=0))
-        found = mm(t_high, bv_high[:, columns]) + (mm(t_low, bv_high[:, columns]) + mm(t_high, bv_low[:, columns]))
+            denom = jnp.sum(jnp.where(lane == 200, total, 0.0), axis=1, keepdims=True)
+            halves.append((total * (1.0 / denom)).astype(BF16))
+        found = mm(jnp.concatenate(halves, axis=0), bv[:, columns])
         pieces.append(jnp.where(first_half, found[0:TOK, :], found[TOK : 2 * TOK, :]))
     attended = jnp.concatenate(pieces, axis=1).astype(BF16)
-    hidden = hid_ref[...] + mod_ref[2] * mm(attended, wout[...])
-    center = hidden - jnp.mean(hidden, axis=1, keepdims=True)
-    variance = jnp.mean(center * center, axis=1, keepdims=True)
-    final = center * lax.rsqrt(variance + EPSILON) * (1.0 + mod_ref[4]) + mod_ref[3]
-    vel_ref[...] = mm3(head_ref[...], final, mm_nt)
+    width = 256
+    total = jnp.zeros((TOK, 1), F32)
+    for part in range(D // width):
+        columns = slice(part * width, (part + 1) * width)
+        piece = hid_ref[:, columns] + mod_ref[2][:, columns] * mm(attended, wout[:, columns])
+        hid_ref[:, columns] = piece
+        total = total + jnp.sum(piece, axis=1, keepdims=True)
+    mean = total * (1.0 / D)
+    square = jnp.zeros((TOK, 1), F32)
+    velocity = jnp.zeros((LAT, TOK), F32)
+    for part in range(D // width):
+        columns = slice(part * width, (part + 1) * width)
+        center = hid_ref[:, columns] - mean
+        square = square + jnp.sum(center * center, axis=1, keepdims=True)
+        c_high, c_low = split(center)
+        velocity = velocity + (mm_nt(hp_high[:, columns], c_high)
+                               + (mm_nt(hp_high[:, columns], c_low) + mm_nt(hp_low[:, columns], c_high)))
+    inv_dev = jnp.broadcast_to(lax.rsqrt(square * (1.0 / D) + EPSILON), (TOK, TOK)).T[0:1, :]
+    vel_ref[...] = velocity * inv_dev + hp_const[...]
     swap = pltpu.make_async_remote_copy(
         src_ref=vel_ref, dst_ref=vel_in, send_sem=ps_sem, recv_sem=pr_sem,
         device_id={"pair": other}, device_id_type=mesh_ids)
@@ -249,6 +261,8 @@
     owner = iota((3 * N_SEQ, TOK), 0)
     owner = jnp.where(owner < N_SEQ, owner, jnp.where(owner < 2 * N_SEQ, owner - N_SEQ - 1, owner - 2 * N_SEQ + 1))
     dispatch = jnp.where(own96 == owner, 1.0, 0.0).astype(BF16)
+    for shift in range(1, N_SEQ):
+        g_copy(shift).wait_send()
     swap.wait()
     mine, theirs = vel_ref[...], vel_in[...]
     is_cond = pair == 0
@@ -262,21 +276,27 @@
         iota((N_SEQ, TOK), 1) < LAT * CAP, packed[0:N_SEQ, :], packed[N_SEQ : 2 * N_SEQ, :])
     sendbuf[:, 1, :] = packed[2 * N_SEQ :, :]
 
-    keep = pltpu.make_async_copy(sendbuf.at[me], rbuf.at[me], lsem.at[12])
-    keep.start()
     for shift in range(1, N_SEQ):
         dest = (me + shift) % N_SEQ
         pltpu.make_async_remote_copy(
             src_ref=sendbuf.at[dest], dst_ref=rbuf.at[me], send_sem=as_sem.at[shift], recv_sem=ar_sem.at[shift],
             device_id={"seq": dest}, device_id_type=mesh_ids).start()
+    keep = pltpu.make_async_copy(sendbuf.at[me], rbuf.at[me], lsem.at[14])
+    keep.start()
 
     lower = jnp.maximum(me - 1, 0)
     upper = jnp.minimum(me + 1, N_SEQ - 1)
     nb_ref[0:1, :] = gath[lower].astype(F32)[11:12, :]
     nb_ref[1:2, :] = gath[upper].astype(F32)[11:12, :]
     nb_ref[2:8, :] = jnp.zeros((6, TOK), F32)
-    for shift in range(1, N_SEQ):
-        g_copy(shift).wait_send()
+    loads[12].wait()
+    index = km_ref[...]
+    index = jnp.where(index < SLOTS, ((index & (CAP - 1)) << 5) + (index >> 3), index)
+    spot_ref[...] = index & (TOK - 1)
+    chunk_ref[...] = index >> 7
+    near_ref[...] = jnp.minimum(index, 300).astype(F32)
+    far_ref[...] = jnp.where(index >= SLOTS, jnp.minimum(index - SLOTS, 300), 300).astype(F32)
+    loads[13].wait()
     keep.wait()
     for shift in range(1, N_SEQ):
         source = (me + N_SEQ - shift) % N_SEQ
@@ -293,15 +313,11 @@
 
 
 def conv_kernel(
-    x_ref, nb_ref, km_hbm, dproj_hbm, wt_hbm, owned_ref, dec_ref, km_ref, dproj_ref, wt, feats, spot_ref, chunk_ref,
-    near_ref, far_ref, prod_a, prod_b, acc_x, acc_m, lsem
+    x_ref, nb_ref, wt, spot_ref, chunk_ref, near_ref, far_ref, dproj_hbm, owned_ref, dec_ref, dproj_ref, feats, prod_a,
+    prod_b, acc_x, acc_m, lsem
 ):
-    loads = [
-        pltpu.make_async_copy(source, target, lsem.at[number])
-        for number, (source, target) in enumerate(((dproj_hbm, dproj_ref), (km_hbm, km_ref), (wt_hbm, wt)))
-    ]
-    for load in loads:
-        load.start()
+    load = pltpu.make_async_copy(dproj_hbm, dproj_ref, lsem)
+    load.start()
     x0 = x_ref[:, 0, :]
     x1 = x_ref[:, 1, :]
 
@@ -330,7 +346,7 @@
         offset = CAP if side == 0 else 0
         parts.append(jnp.where(lane // LAT == sub % CAP + offset, rows, 0.0))
     l_high, l_low = split(jnp.concatenate(parts, axis=0))
-    loads[0].wait()
+    load.wait()
     p_high, p_low = split(dproj_ref[...])
     p_high = jnp.concatenate([p_high.astype(F32)] * (TOK // LAT), axis=0).astype(BF16)
     p_low = jnp.concatenate([p_low.astype(F32)] * (TOK // LAT), axis=0).astype(BF16)
@@ -339,14 +355,6 @@
     feats[...] = (half * jnp.tanh(half) + half).astype(BF16)
     acc_x[...] = jnp.zeros((OUT_DEV, FINE), F32)
     acc_m[...] = jnp.zeros((OUT_DEV, FINE), F32)
-    loads[1].wait()
-    index = km_ref[...]
-    index = jnp.where(index < SLOTS, ((index & (CAP - 1)) << 5) + (index >> 3), index)
-    spot_ref[...] = index & (TOK - 1)
-    chunk_ref[...] = index >> 7
-    near_ref[...] = jnp.minimum(index, 300).astype(F32)
-    far_ref[...] = jnp.where(index >= SLOTS, jnp.minimum(index - SLOTS, 300), 300).astype(F32)
-    loads[2].wait()
 
     def product(part, half, target):
         rows = pl.ds(pl.multiple_of(part * (TRIPLE * OUT_DEV), TRIPLE * OUT_DEV), TRIPLE * OUT_DEV)
@@ -409,6 +417,10 @@
     return [pl.BlockSpec(memory_space=pltpu.VMEM)] * count
 
 
+def in_hbm(*arrays):
+    return [pltpu.with_memory_space_constraint(array, pltpu.HBM) for array in arrays]
+
+
 def hbm(count):
     return [pl.BlockSpec(memory_space=pltpu.HBM)] * count
 
@@ -421,11 +433,15 @@
     table_high = table.astype(jnp.bfloat16)
     table_low = (table - table_high.astype(np.float32)).astype(jnp.bfloat16)
     dma = pltpu.SemaphoreType.DMA
-    gathered, borders = pl.pallas_call(
+    conv_table = jax.ShapeDtypeStruct((KOFF, BLOCKS, TOK), jnp.int32)
+    conv_row = jax.ShapeDtypeStruct((KOFF, BLOCKS, TOK), F32)
+    handed = pl.pallas_call(
         flow_kernel,
-        out_shape=(jax.ShapeDtypeStruct((N_SEQ, 2, TOK), F32), jax.ShapeDtypeStruct((8, TOK), F32)),
-        in_specs=hbm(3) + [pl.BlockSpec(memory_space=pltpu.SMEM)] + hbm(9),
-        out_specs=tuple(vmem(2)),
+        out_shape=(
+            jax.ShapeDtypeStruct((N_SEQ, 2, TOK), F32), jax.ShapeDtypeStruct((8, TOK), F32),
+            jax.ShapeDtypeStruct((KOFF * OUT_DEV, DEC), BF16), conv_table, conv_table, conv_row, conv_row),
+        in_specs=hbm(3) + [pl.BlockSpec(memory_space=pltpu.SMEM)] + hbm(11),
+        out_specs=tuple(vmem(7)),
         scratch_shapes=[
             pltpu.VMEM((LAT, TOK), F32),
             pltpu.VMEM((3, 1, TOK), jnp.int32),
@@ -439,52 +455,52 @@
             pltpu.VMEM((3 * RES, D), BF16),
             pltpu.VMEM((D, 3 * HW), BF16),
             pltpu.VMEM((HW, D), BF16),
+            pltpu.VMEM((KOFF, BLOCKS, TOK), jnp.int32),
             pltpu.VMEM((N_SEQ, 16, TOK), BF16),
             pltpu.VMEM((16, TOK), F32),
+            pltpu.VMEM((FEAT, D), BF16),
             pltpu.VMEM((HW, FEAT), BF16),
-            pltpu.VMEM((FEAT, HW), BF16),
             pltpu.VMEM((FEAT, HW), BF16),
             pltpu.VMEM((HEADS * TOK, FEAT), BF16),
             pltpu.VMEM((TOK, D), F32),
-            pltpu.VMEM((FEAT, GROUP), BF16),
-            pltpu.VMEM((HEADS * TOK, GROUP), BF16),
+            pltpu.VMEM((FEAT, 2 * GROUP), BF16),
+            pltpu.VMEM((FEAT, 2 * GROUP), BF16),
+            pltpu.VMEM((HEADS * TOK, 2 * GROUP), BF16),
             pltpu.VMEM((HEADS * TOK, FEAT), F32),
+            pltpu.VMEM((LAT, D), BF16),
+            pltpu.VMEM((LAT, D), BF16),
+            pltpu.VMEM((LAT, TOK), F32),
             pltpu.VMEM((LAT, TOK), F32),
             pltpu.VMEM((LAT, TOK), F32),
             pltpu.VMEM((N_SEQ, 2, TOK), F32),
             pltpu.VMEM((N_SEQ, 2, TOK), F32),
-            dma((13,)), dma((N_SEQ,)), dma((N_SEQ,)), dma, dma, dma((N_SEQ,)), dma((N_SEQ,)),
+            dma((15,)), dma((N_SEQ,)), dma((N_SEQ,)), dma, dma, dma((N_SEQ,)), dma((N_SEQ,)),
         ],
-        compiler_params=pltpu.CompilerParams(collective_id=0, has_side_effects=True, vmem_limit_bytes=67043328),
+        compiler_params=pltpu.CompilerParams(collective_id=0, has_side_effects=True, vmem_limit_bytes=40 << 20),
         name="flow",
-    )(
-        latents[0], jnp.transpose(voxel_coords, (1, 0, 2)), owner_map.reshape(1, TOK), step_time,
+    )(*in_hbm(
+        latents[0], jnp.transpose(voxel_coords, (1, 0, 2)), owner_map.reshape(1, TOK)), step_time, *in_hbm(
         modulation.reshape(5, 1, D), in_proj, norm_gain, head_proj.T, border_blocks[0, 0], jnp.asarray(table_high),
         jnp.asarray(table_low), qkv_proj, out_proj,
+        jnp.swapaxes(conv_weight, 1, 2).reshape(KOFF * OUT_DEV, DEC), kernel_map.reshape(KOFF, BLOCKS, TOK)),
     )
     owned, decoded = pl.pallas_call(
         conv_kernel,
         out_shape=(jax.ShapeDtypeStruct((LAT, SLOTS), F32), jax.ShapeDtypeStruct((OUT_DEV, FINE), BF16)),
-        in_specs=vmem(2) + hbm(3),
+        in_specs=vmem(7) + hbm(1),
         out_specs=tuple(vmem(2)),
         scratch_shapes=[
-            pltpu.VMEM((KOFF, BLOCKS, TOK), jnp.int32),
             pltpu.VMEM((LAT, DEC), F32),
-            pltpu.VMEM((KOFF * OUT_DEV, DEC), BF16),
             pltpu.VMEM((2 * SLOTS, DEC), BF16),
-            pltpu.VMEM((KOFF, BLOCKS, TOK), jnp.int32),
-            pltpu.VMEM((KOFF, BLOCKS, TOK), jnp.int32),
-            pltpu.VMEM((KOFF, BLOCKS, TOK), F32),
-            pltpu.VMEM((KOFF, BLOCKS, TOK), F32),
             pltpu.VMEM((TRIPLE * OUT_DEV, 2 * SLOTS), F32),
             pltpu.VMEM((TRIPLE * OUT_DEV, 2 * SLOTS), F32),
             pltpu.VMEM((OUT_DEV, FINE), F32),
             pltpu.VMEM((OUT_DEV, FINE), F32),
-            dma((3,)),
+            dma,
         ],
-        compiler_params=pltpu.CompilerParams(vmem_limit_bytes=67043328),
+        compiler_params=pltpu.CompilerParams(vmem_limit_bytes=40 << 20),
         name="conv",
-    )(gathered, borders, kernel_map.reshape(KOFF, BLOCKS, TOK), decoder_projection, jnp.swapaxes(conv_weight, 1, 2).reshape(KOFF * OUT_DEV, DEC))
+    )(*handed, *in_hbm(decoder_projection))
     return owned[None, None], decoded.T[None, None]
 
 

time: 45.4 us -> 42.5 us (0.936)
  Pallas kernels: 43.9 us -> 41.1 us
    pallas_call x1, Pallas kernels: 10.3 us -> 8.77 us  [per_device(): pl.pallas_call(conv_kernel, out_shape=(jax.ShapeDtypeStruct((LAT, SLOTS),...]
    pallas_call x1, Pallas kernels: 33.6 us -> 32.3 us  [per_device(): pl.pallas_call(flow_kernel, out_shape=(jax.ShapeDtypeStruct((N_SEQ, 2, TO...]
where the time goes in v4:
time: 42.5 us; the launch traced here: 42.4 us
  Pallas kernels  41.1 us (97%)
  between operations  1.29 us (3%)
    pallas_call x1, Pallas kernels, per_device(): pl.pallas_call(flow_kernel, out_shape=(jax.ShapeDtypeStruct((N_SEQ, 2, TO...  32.3 us
    pallas_call x1, Pallas kernels, per_device(): pl.pallas_call(conv_kernel, out_shape=(jax.ShapeDtypeStruct((LAT, SLOTS),...  8.77 us

profile of v4, /device:TPU:1, one launch (start us, length us, event | category | flops | bytes accessed | tf_op | source)
XLA Modules:
  0.0 42.4 jit_solution(10248570524907495956)
XLA Ops:
  1.3 32.3 %flow.1 = (f32[32,2,128]{2,1,0:T(2,128)S(1)}, f32[8,128]{1,0:T(8,128)S(1)}, bf16[2592,768]{1,0:T(8,128)(2,1)S(1)}, s32[27,8,128]{2,1,0:T(8,128)S(1)}, s32[27,8,1...) custom-call(f32[8,128]{1,0:T(8,128)} %bitcast.18, s32[3,1,128]{2,1,0:T(1,128)} %bitcast.19, ...), custom_call_target="tpu_custom_call" | custom-call | tf_op jit(solution)/shard_map/flow/pallas_call | solution.py:438
  33.6 8.8 %conv.1 = (f32[8,256]{1,0:T(8,128)}, bf16[96,1024]{1,0:T(8,128)(2,1)}) custom-call(f32[32,2,128]{2,1,0:T(2,128)S(1)} %get-tuple-element.11.x_ref, f32[8,128]{1,0:T(8,128)S(1)} %get-tuple-element.12.nb_ref, bf16[2592,768]{1,0:T(8,128)(2,1)S(1)} %get-tuple-element.13.wt, s32[27,8,128]{2,1,0:T(8,128)S(1)} %get-tuple-element.14.spot_ref, ...), custom_call_target="tpu_custom_call" | custom-call | tf_op jit(solution)/shard_map/conv/pallas_call | solution.py:487

commit v5 on v4

--- a/solution.py
+++ b/solution.py
@@ -28,6 +28,7 @@
 OUT_DEV = 96
 GROUP = NX * TOK
 FEAT = 256
+TILES = ((0,), (1, 7), (2, 6), (3, 5), (4,))
 EPSILON = 1e-06
 GUIDANCE = 3.0
 LOG2E = 1.4426950408889634
@@ -162,57 +163,59 @@
     head_scaled = head_ref[...] * (1.0 + mod_ref[4])
     hp_high[...], hp_low[...] = split(head_scaled)
     hp_const[...] = jnp.broadcast_to(jnp.sum(head_ref[...] * mod_ref[3], axis=1, keepdims=True), (LAT, TOK))
-    acc[...] = jnp.zeros((HEADS * TOK, FEAT), F32)
     loads[12].start()
     loads[13].start()
 
-    def arrived(z_back, first):
+    def features(number):
         sources = []
-        z_from = (z_me + NZ - z_back) % NZ
-        for x_back in range(NX):
-            source = ((x_me + NX - x_back) % NX) * NZ + z_from
-            shift = (me + N_SEQ - source) % N_SEQ
-            sources.append(source)
-
-            def wait():
-                pltpu.make_async_remote_copy(
-                    src_ref=gath.at[source], dst_ref=gath.at[source], send_sem=gs_sem.at[shift],
-                    recv_sem=gr_sem.at[shift], device_id={"seq": me}, device_id_type=mesh_ids).wait_recv()
-
-            if x_back == 0 and first is not None:
-                pl.when(first)(wait)
-            else:
-                wait()
-        return sources
-
-    def one_group(step, carry):
-        sources = arrived((NZ - step) % NZ, step > 0) + arrived(step + 1, None)
+        for z_back in TILES[number]:
+            for x_back in range(NX):
+                source = ((x_me + NX - x_back) % NX) * NZ + (z_me + NZ - z_back) % NZ
+                shift = (me + N_SEQ - source) % N_SEQ
+                sources.append(source)
+                if x_back > 0 or z_back > 0:
+                    pltpu.make_async_remote_copy(
+                        src_ref=gath.at[source], dst_ref=gath.at[source], send_sem=gs_sem.at[shift],
+                        recv_sem=gr_sem.at[shift], device_id={"seq": me}, device_id_type=mesh_ids).wait_recv()
+        width = TOK * len(sources)
         rows = jnp.concatenate([gath[source].astype(F32) for source in sources], axis=1)
         std_high, std_low = rows[12:13, :], rows[13:14, :]
         std = std_high + std_low
         inv_std = 1.0 / std
-        which = iota((8, 2 * GROUP), 0)
-        ids = iota((RES, 2 * GROUP), 0).astype(F32)
+        which = iota((8, width), 0)
+        ids = iota((RES, width), 0).astype(F32)
+        ft, fs = ft_ref.at[number % 2], fs_ref.at[number % 2]
         for c in range(3):
             hit = ids == rows[8 + c : 9 + c, :]
-            ft_ref[c * RES : (c + 1) * RES, :] = jnp.where(hit, 1.0, 0.0).astype(BF16)
-            fs_ref[c * RES : (c + 1) * RES, :] = jnp.where(hit, inv_std, 0.0).astype(BF16)
+            ft[c * RES : (c + 1) * RES, 0:width] = jnp.where(hit, 1.0, 0.0).astype(BF16)
+            fs[c * RES : (c + 1) * RES, 0:width] = jnp.where(hit, inv_std, 0.0).astype(BF16)
         std_rows = jnp.where(which == 0, std_high, jnp.where(which == 1, std_low, 0.0))
-        pad = jnp.zeros((48, 2 * GROUP), F32)
-        ft_ref[3 * RES :, :] = jnp.concatenate([rows[0:8, :], std_rows, pad], axis=0).astype(BF16)
-        fs_ref[3 * RES :, :] = jnp.concatenate(
+        pad = jnp.zeros((48, width), F32)
+        ft[3 * RES :, 0:width] = jnp.concatenate([rows[0:8, :], std_rows, pad], axis=0).astype(BF16)
+        fs[3 * RES :, 0:width] = jnp.concatenate(
             [rows[0:8, :] * inv_std, jnp.where(which == 0, 1.0, 0.0), pad], axis=0).astype(BF16)
-        keys = mm(bkt[...], ft_ref[...])
-        scores = mm(umat[...], ft_ref[...])
+        return width, EPSILON * (std * std)
+
+    width, eps_var = features(0)
+    for number in range(len(TILES)):
+        ft, fs = ft_ref[number % 2, :, 0:width], fs_ref[number % 2, :, 0:width]
+        used, used_var = width, eps_var
+        if 2 <= number < len(TILES) - 1:
+            width, eps_var = features(number + 1)
+        keys = mm(bkt[...], ft)
+        scores = mm(umat[...], ft)
         for head in range(HEADS):
             keys_h = keys[head * HEAD : (head + 1) * HEAD, :]
             mean_h = jnp.sum(keys_h * keys_h, axis=0, keepdims=True) * (1.0 / HEAD)
-            inv = lax.rsqrt(mean_h + EPSILON * (std * std))
-            p_ref[head * TOK : (head + 1) * TOK, :] = jnp.exp2(scores[head * TOK : (head + 1) * TOK, :] * inv).astype(BF16)
-        acc[...] += mm_nt(p_ref[...], fs_ref[...])
-        return carry
-
-    lax.fori_loop(0, NZ // 2, one_group, 0)
+            inv = lax.rsqrt(mean_h + used_var)
+            p_ref[head * TOK : (head + 1) * TOK, 0:used] = jnp.exp2(
+                scores[head * TOK : (head + 1) * TOK, :] * inv).astype(BF16)
+        if number < 2:
+            width, eps_var = features(number + 1)
+        found = mm_nt(p_ref[:, 0:used], fs)
+        if number > 0:
+            found += acc[...]
+        acc[...] = found
 
     loads[11].wait()
     lane = iota((TOK, FEAT), 1)
@@ -463,8 +466,8 @@
             pltpu.VMEM((FEAT, HW), BF16),
             pltpu.VMEM((HEADS * TOK, FEAT), BF16),
             pltpu.VMEM((TOK, D), F32),
-            pltpu.VMEM((FEAT, 2 * GROUP), BF16),
-            pltpu.VMEM((FEAT, 2 * GROUP), BF16),
+            pltpu.VMEM((2, FEAT, 2 * GROUP), BF16),
+            pltpu.VMEM((2, FEAT, 2 * GROUP), BF16),
             pltpu.VMEM((HEADS * TOK, 2 * GROUP), BF16),
             pltpu.VMEM((HEADS * TOK, FEAT), F32),
             pltpu.VMEM((LAT, D), BF16),

time: 42.5 us -> 42.8 us (level)
  no operation moved by 1% of the time
where the time goes in v5:
time: 42.8 us; the launch traced here: 42.7 us
  Pallas kernels  41.4 us (97%)
  between operations  1.29 us (3%)
    pallas_call x1, Pallas kernels, per_device(): pl.pallas_call(flow_kernel, out_shape=(jax.ShapeDtypeStruct((N_SEQ, 2, TO...  32.6 us
    pallas_call x1, Pallas kernels, per_device(): pl.pallas_call(conv_kernel, out_shape=(jax.ShapeDtypeStruct((LAT, SLOTS),...  8.77 us

profile of v5, /device:TPU:1, one launch (start us, length us, event | category | flops | bytes accessed | tf_op | source)
XLA Modules:
  0.0 42.7 jit_solution(9224150068965272480)
XLA Ops:
  1.3 32.6 %flow.1 = (f32[32,2,128]{2,1,0:T(2,128)S(1)}, f32[8,128]{1,0:T(8,128)S(1)}, bf16[2592,768]{1,0:T(8,128)(2,1)S(1)}, s32[27,8,128]{2,1,0:T(8,128)S(1)}, s32[27,8,1...) custom-call(f32[8,128]{1,0:T(8,128)} %bitcast.18, s32[3,1,128]{2,1,0:T(1,128)} %bitcast.19, ...), custom_call_target="tpu_custom_call" | custom-call | tf_op jit(solution)/shard_map/flow/pallas_call | solution.py:441
  33.9 8.8 %conv.1 = (f32[8,256]{1,0:T(8,128)}, bf16[96,1024]{1,0:T(8,128)(2,1)}) custom-call(f32[32,2,128]{2,1,0:T(2,128)S(1)} %get-tuple-element.11.x_ref, f32[8,128]{1,0:T(8,128)S(1)} %get-tuple-element.12.nb_ref, bf16[2592,768]{1,0:T(8,128)(2,1)S(1)} %get-tuple-element.13.wt, s32[27,8,128]{2,1,0:T(8,128)S(1)} %get-tuple-element.14.spot_ref, ...), custom_call_target="tpu_custom_call" | custom-call | tf_op jit(solution)/shard_map/conv/pallas_call | solution.py:490

commit v6 on v5

--- a/solution.py
+++ b/solution.py
@@ -29,6 +29,7 @@
 GROUP = NX * TOK
 FEAT = 256
 TILES = ((0,), (1, 7), (2, 6), (3, 5), (4,))
+HOPS = (4, 3)
 EPSILON = 1e-06
 GUIDANCE = 3.0
 LOG2E = 1.4426950408889634
@@ -76,7 +77,7 @@
     lat_ref, coord_ref, own_ref, mod_ref, inp_ref, gain_ref, head_ref, bb_ref, tabh, tabl, wqkv, wout, km_ref,
     gath, stage, scaled, bkt, bv, umat, hid_ref, ft_ref, fs_ref, p_ref, acc, hp_high, hp_low, hp_const, vel_ref, vel_in,
     sendbuf, rbuf,
-    lsem, gs_sem, gr_sem, ps_sem, pr_sem, as_sem, ar_sem,
+    lsem, xs_sem, xr_sem, zs_sem, zr_sem, ps_sem, pr_sem, as_sem, ar_sem,
 ):
     me = lax.axis_index("seq")
     pair = lax.axis_index("pair")
@@ -96,8 +97,10 @@
         load.start()
 
     barrier = pltpu.get_barrier_semaphore()
-    for shift in range(1, N_SEQ):
-        pl.semaphore_signal(barrier, inc=1, device_id={"seq": (me + shift) % N_SEQ}, device_id_type=mesh_ids)
+    up, down = (z_me + 1) % NZ, (z_me + NZ - 1) % NZ
+    near = [((x_me + shift) % NX) * NZ + z_me for shift in range(1, NX)] + [x_me * NZ + up, x_me * NZ + down]
+    for peer in near:
+        pl.semaphore_signal(barrier, inc=1, device_id={"seq": peer}, device_id_type=mesh_ids)
     pl.semaphore_signal(barrier, inc=1, device_id={"pair": other}, device_id_type=mesh_ids)
     for load in loads[:10]:
         load.wait()
@@ -128,16 +131,30 @@
     std_high = std.astype(BF16).astype(F32)
     stage[12:13, :] = std_high
     stage[13:14, :] = std - std_high
-    gath[me] = stage[...].astype(BF16)
-
-    def g_copy(shift):
+    gath[z_me, x_me] = stage[...].astype(BF16)
+
+    def x_copy(shift):
         return pltpu.make_async_remote_copy(
-            src_ref=gath.at[me], dst_ref=gath.at[me], send_sem=gs_sem.at[shift], recv_sem=gr_sem.at[shift],
-            device_id={"seq": (me + shift) % N_SEQ}, device_id_type=mesh_ids)
-
-    pl.semaphore_wait(barrier, N_SEQ)
-    for shift in range(1, N_SEQ):
-        g_copy(shift).start()
+            src_ref=gath.at[z_me, x_me], dst_ref=gath.at[z_me, x_me], send_sem=xs_sem.at[shift - 1],
+            recv_sem=xr_sem.at[shift - 1], device_id={"seq": near[shift - 1]}, device_id_type=mesh_ids)
+
+    def x_arrival(shift):
+        source = (x_me + NX - shift) % NX
+        return pltpu.make_async_remote_copy(
+            src_ref=gath.at[z_me, source], dst_ref=gath.at[z_me, source], send_sem=xs_sem.at[shift - 1],
+            recv_sem=xr_sem.at[shift - 1], device_id={"seq": me}, device_id_type=mesh_ids)
+
+    def z_copy(way, hop, arriving=False):
+        gone = hop if arriving else hop - 1
+        block = (z_me + NZ - gone) % NZ if way == 0 else (z_me + gone) % NZ
+        return pltpu.make_async_remote_copy(
+            src_ref=gath.at[block], dst_ref=gath.at[block], send_sem=zs_sem.at[way, hop - 1],
+            recv_sem=zr_sem.at[way, hop - 1], device_id={"seq": me if arriving else near[3 + way]},
+            device_id_type=mesh_ids)
+
+    pl.semaphore_wait(barrier, len(near) + 1)
+    for shift in range(1, NX):
+        x_copy(shift).start()
 
     scale1 = 1.0 + mod_ref[1]
     normed = (center * lax.rsqrt(variance + EPSILON) * scale1 + mod_ref[0]).astype(BF16)
@@ -167,18 +184,17 @@
     loads[13].start()
 
     def features(number):
-        sources = []
-        for z_back in TILES[number]:
-            for x_back in range(NX):
-                source = ((x_me + NX - x_back) % NX) * NZ + (z_me + NZ - z_back) % NZ
-                shift = (me + N_SEQ - source) % N_SEQ
-                sources.append(source)
-                if x_back > 0 or z_back > 0:
-                    pltpu.make_async_remote_copy(
-                        src_ref=gath.at[source], dst_ref=gath.at[source], send_sem=gs_sem.at[shift],
-                        recv_sem=gr_sem.at[shift], device_id={"seq": me}, device_id_type=mesh_ids).wait_recv()
+        if number == 0:
+            for shift in range(1, NX):
+                x_arrival(shift).wait_recv()
+        for way in range(2):
+            if number > 0 and number <= HOPS[way]:
+                z_copy(way, number, True).wait_recv()
+            if number < HOPS[way]:
+                z_copy(way, number + 1).start()
+        sources = [((z_me + z) % NZ, x) for z in TILES[number] for x in range(NX)]
         width = TOK * len(sources)
-        rows = jnp.concatenate([gath[source].astype(F32) for source in sources], axis=1)
+        rows = jnp.concatenate([gath[z, x].astype(F32) for z, x in sources], axis=1)
         std_high, std_low = rows[12:13, :], rows[13:14, :]
         std = std_high + std_low
         inv_std = 1.0 / std
@@ -200,8 +216,6 @@
     for number in range(len(TILES)):
         ft, fs = ft_ref[number % 2, :, 0:width], fs_ref[number % 2, :, 0:width]
         used, used_var = width, eps_var
-        if 2 <= number < len(TILES) - 1:
-            width, eps_var = features(number + 1)
         keys = mm(bkt[...], ft)
         scores = mm(umat[...], ft)
         for head in range(HEADS):
@@ -210,7 +224,7 @@
             inv = lax.rsqrt(mean_h + used_var)
             p_ref[head * TOK : (head + 1) * TOK, 0:used] = jnp.exp2(
                 scores[head * TOK : (head + 1) * TOK, :] * inv).astype(BF16)
-        if number < 2:
+        if number + 1 < len(TILES):
             width, eps_var = features(number + 1)
         found = mm_nt(p_ref[:, 0:used], fs)
         if number > 0:
@@ -264,8 +278,11 @@
     owner = iota((3 * N_SEQ, TOK), 0)
     owner = jnp.where(owner < N_SEQ, owner, jnp.where(owner < 2 * N_SEQ, owner - N_SEQ - 1, owner - 2 * N_SEQ + 1))
     dispatch = jnp.where(own96 == owner, 1.0, 0.0).astype(BF16)
-    for shift in range(1, N_SEQ):
-        g_copy(shift).wait_send()
+    for shift in range(1, NX):
+        x_copy(shift).wait_send()
+    for way in range(2):
+        for hop in range(1, HOPS[way] + 1):
+            z_copy(way, hop).wait_send()
     swap.wait()
     mine, theirs = vel_ref[...], vel_in[...]
     is_cond = pair == 0
@@ -289,8 +306,8 @@
 
     lower = jnp.maximum(me - 1, 0)
     upper = jnp.minimum(me + 1, N_SEQ - 1)
-    nb_ref[0:1, :] = gath[lower].astype(F32)[11:12, :]
-    nb_ref[1:2, :] = gath[upper].astype(F32)[11:12, :]
+    nb_ref[0:1, :] = gath[lower % NZ, lower // NZ].astype(F32)[11:12, :]
+    nb_ref[1:2, :] = gath[upper % NZ, upper // NZ].astype(F32)[11:12, :]
     nb_ref[2:8, :] = jnp.zeros((6, TOK), F32)
     loads[12].wait()
     index = km_ref[...]
@@ -459,7 +476,7 @@
             pltpu.VMEM((D, 3 * HW), BF16),
             pltpu.VMEM((HW, D), BF16),
             pltpu.VMEM((KOFF, BLOCKS, TOK), jnp.int32),
-            pltpu.VMEM((N_SEQ, 16, TOK), BF16),
+            pltpu.VMEM((NZ, NX, 16, TOK), BF16),
             pltpu.VMEM((16, TOK), F32),
             pltpu.VMEM((FEAT, D), BF16),
             pltpu.VMEM((HW, FEAT), BF16),
@@ -477,7 +494,7 @@
             pltpu.VMEM((LAT, TOK), F32),
             pltpu.VMEM((N_SEQ, 2, TOK), F32),
             pltpu.VMEM((N_SEQ, 2, TOK), F32),
-            dma((15,)), dma((N_SEQ,)), dma((N_SEQ,)), dma, dma, dma((N_SEQ,)), dma((N_SEQ,)),
+            dma((15,)), dma((NX - 1,)), dma((NX - 1,)), dma((2, 4)), dma((2, 4)), dma, dma, dma((N_SEQ,)), dma((N_SEQ,)),
         ],
         compiler_params=pltpu.CompilerParams(collective_id=0, has_side_effects=True, vmem_limit_bytes=40 << 20),
         name="flow",

time: 42.8 us -> 43.5 us (1.016)
  Pallas kernels: 41.4 us -> 42 us
    pallas_call x1, Pallas kernels: 32.6 us -> 33.3 us  [per_device(): pl.pallas_call(flow_kernel, out_shape=(jax.ShapeDtypeStruct((N_SEQ, 2, TO...]
where the time goes in v6:
time: 43.5 us; the launch traced here: 43.3 us
  Pallas kernels  42 us (97%)
  between operations  1.29 us (3%)
    pallas_call x1, Pallas kernels, per_device(): pl.pallas_call(flow_kernel, out_shape=(jax.ShapeDtypeStruct((N_SEQ, 2, TO...  33.3 us
    pallas_call x1, Pallas kernels, per_device(): pl.pallas_call(conv_kernel, out_shape=(jax.ShapeDtypeStruct((LAT, SLOTS),...  8.76 us

profile of v6, /device:TPU:1, one launch (start us, length us, event | category | flops | bytes accessed | tf_op | source)
XLA Modules:
  0.0 43.3 jit_solution(9829134696454632312)
XLA Ops:
  1.3 33.3 %flow.1 = (f32[32,2,128]{2,1,0:T(2,128)S(1)}, f32[8,128]{1,0:T(8,128)S(1)}, bf16[2592,768]{1,0:T(8,128)(2,1)S(1)}, s32[27,8,128]{2,1,0:T(8,128)S(1)}, s32[27,8,1...) custom-call(f32[8,128]{1,0:T(8,128)} %bitcast.18, s32[3,1,128]{2,1,0:T(1,128)} %bitcast.19, ...), custom_call_target="tpu_custom_call" | custom-call | tf_op jit(solution)/shard_map/flow/pallas_call | solution.py:458
  34.6 8.8 %conv.1 = (f32[8,256]{1,0:T(8,128)}, bf16[96,1024]{1,0:T(8,128)(2,1)}) custom-call(f32[32,2,128]{2,1,0:T(2,128)S(1)} %get-tuple-element.11.x_ref, f32[8,128]{1,0:T(8,128)S(1)} %get-tuple-element.12.nb_ref, bf16[2592,768]{1,0:T(8,128)(2,1)S(1)} %get-tuple-element.13.wt, s32[27,8,128]{2,1,0:T(8,128)S(1)} %get-tuple-element.14.spot_ref, ...), custom_call_target="tpu_custom_call" | custom-call | tf_op jit(solution)/shard_map/conv/pallas_call | solution.py:507

commit v7 on v5

--- a/solution.py
+++ b/solution.py
@@ -29,6 +29,7 @@
 GROUP = NX * TOK
 FEAT = 256
 TILES = ((0,), (1, 7), (2, 6), (3, 5), (4,))
+NEAR_FIRST = tuple((dx, dz) for tile in TILES for dx in (0, 1, 3, 2) for dz in tile if dx or dz)
 EPSILON = 1e-06
 GUIDANCE = 3.0
 LOG2E = 1.4426950408889634
@@ -85,6 +86,12 @@
     z_me = me % NZ
     mesh_ids = pl.DeviceIdType.MESH
 
+    def ahead(dx, dz):
+        return ((x_me + dx) % NX) * NZ + (z_me + dz) % NZ
+
+    def behind(dx, dz):
+        return ((x_me + NX - dx) % NX) * NZ + (z_me + NZ - dz) % NZ
+
     loads = [
         pltpu.make_async_copy(source, target, lsem.at[number])
         for number, (source, target) in enumerate((
@@ -96,8 +103,8 @@
         load.start()
 
     barrier = pltpu.get_barrier_semaphore()
-    for shift in range(1, N_SEQ):
-        pl.semaphore_signal(barrier, inc=1, device_id={"seq": (me + shift) % N_SEQ}, device_id_type=mesh_ids)
+    for dx, dz in reversed(NEAR_FIRST):
+        pl.semaphore_signal(barrier, inc=1, device_id={"seq": ahead(dx, dz)}, device_id_type=mesh_ids)
     pl.semaphore_signal(barrier, inc=1, device_id={"pair": other}, device_id_type=mesh_ids)
     for load in loads[:10]:
         load.wait()
@@ -130,14 +137,14 @@
     stage[13:14, :] = std - std_high
     gath[me] = stage[...].astype(BF16)
 
-    def g_copy(shift):
+    def g_copy(dx, dz):
         return pltpu.make_async_remote_copy(
-            src_ref=gath.at[me], dst_ref=gath.at[me], send_sem=gs_sem.at[shift], recv_sem=gr_sem.at[shift],
-            device_id={"seq": (me + shift) % N_SEQ}, device_id_type=mesh_ids)
+            src_ref=gath.at[me], dst_ref=gath.at[me], send_sem=gs_sem.at[dx, dz], recv_sem=gr_sem.at[dx, dz],
+            device_id={"seq": ahead(dx, dz)}, device_id_type=mesh_ids)
 
     pl.semaphore_wait(barrier, N_SEQ)
-    for shift in range(1, N_SEQ):
-        g_copy(shift).start()
+    for dx, dz in NEAR_FIRST:
+        g_copy(dx, dz).start()
 
     scale1 = 1.0 + mod_ref[1]
     normed = (center * lax.rsqrt(variance + EPSILON) * scale1 + mod_ref[0]).astype(BF16)
@@ -168,15 +175,14 @@
 
     def features(number):
         sources = []
-        for z_back in TILES[number]:
-            for x_back in range(NX):
-                source = ((x_me + NX - x_back) % NX) * NZ + (z_me + NZ - z_back) % NZ
-                shift = (me + N_SEQ - source) % N_SEQ
+        for dz in TILES[number]:
+            for dx in range(NX):
+                source = behind(dx, dz)
                 sources.append(source)
-                if x_back > 0 or z_back > 0:
+                if dx > 0 or dz > 0:
                     pltpu.make_async_remote_copy(
-                        src_ref=gath.at[source], dst_ref=gath.at[source], send_sem=gs_sem.at[shift],
-                        recv_sem=gr_sem.at[shift], device_id={"seq": me}, device_id_type=mesh_ids).wait_recv()
+                        src_ref=gath.at[source], dst_ref=gath.at[source], send_sem=gs_sem.at[dx, dz],
+                        recv_sem=gr_sem.at[dx, dz], device_id={"seq": me}, device_id_type=mesh_ids).wait_recv()
         width = TOK * len(sources)
         rows = jnp.concatenate([gath[source].astype(F32) for source in sources], axis=1)
         std_high, std_low = rows[12:13, :], rows[13:14, :]
@@ -200,8 +206,6 @@
     for number in range(len(TILES)):
         ft, fs = ft_ref[number % 2, :, 0:width], fs_ref[number % 2, :, 0:width]
         used, used_var = width, eps_var
-        if 2 <= number < len(TILES) - 1:
-            width, eps_var = features(number + 1)
         keys = mm(bkt[...], ft)
         scores = mm(umat[...], ft)
         for head in range(HEADS):
@@ -210,7 +214,7 @@
             inv = lax.rsqrt(mean_h + used_var)
             p_ref[head * TOK : (head + 1) * TOK, 0:used] = jnp.exp2(
                 scores[head * TOK : (head + 1) * TOK, :] * inv).astype(BF16)
-        if number < 2:
+        if number + 1 < len(TILES):
             width, eps_var = features(number + 1)
         found = mm_nt(p_ref[:, 0:used], fs)
         if number > 0:
@@ -264,8 +268,8 @@
     owner = iota((3 * N_SEQ, TOK), 0)
     owner = jnp.where(owner < N_SEQ, owner, jnp.where(owner < 2 * N_SEQ, owner - N_SEQ - 1, owner - 2 * N_SEQ + 1))
     dispatch = jnp.where(own96 == owner, 1.0, 0.0).astype(BF16)
-    for shift in range(1, N_SEQ):
-        g_copy(shift).wait_send()
+    for dx, dz in NEAR_FIRST:
+        g_copy(dx, dz).wait_send()
     swap.wait()
     mine, theirs = vel_ref[...], vel_in[...]
     is_cond = pair == 0
@@ -477,7 +481,7 @@
             pltpu.VMEM((LAT, TOK), F32),
             pltpu.VMEM((N_SEQ, 2, TOK), F32),
             pltpu.VMEM((N_SEQ, 2, TOK), F32),
-            dma((15,)), dma((N_SEQ,)), dma((N_SEQ,)), dma, dma, dma((N_SEQ,)), dma((N_SEQ,)),
+            dma((15,)), dma((NX, NZ)), dma((NX, NZ)), dma, dma, dma((N_SEQ,)), dma((N_SEQ,)),
         ],
         compiler_params=pltpu.CompilerParams(collective_id=0, has_side_effects=True, vmem_limit_bytes=40 << 20),
         name="flow",

time: 42.8 us -> 41.1 us (0.960)
  Pallas kernels: 41.4 us -> 39.6 us
    pallas_call x1, Pallas kernels: 32.6 us -> 30.9 us  [per_device(): pl.pallas_call(flow_kernel, out_shape=(jax.ShapeDtypeStruct((N_SEQ, 2, TO...]
where the time goes in v7:
time: 41.1 us; the launch traced here: 40.9 us
  Pallas kernels  39.6 us (96%)
  between operations  1.29 us (3%)
    pallas_call x1, Pallas kernels, per_device(): pl.pallas_call(flow_kernel, out_shape=(jax.ShapeDtypeStruct((N_SEQ, 2, TO...  30.9 us
    pallas_call x1, Pallas kernels, per_device(): pl.pallas_call(conv_kernel, out_shape=(jax.ShapeDtypeStruct((LAT, SLOTS),...  8.77 us

profile of v7, /device:TPU:1, one launch (start us, length us, event | category | flops | bytes accessed | tf_op | source)
XLA Modules:
  0.0 40.9 jit_solution(9650054506714290623)
XLA Ops:
  1.3 30.9 %flow.1 = (f32[32,2,128]{2,1,0:T(2,128)S(1)}, f32[8,128]{1,0:T(8,128)S(1)}, bf16[2592,768]{1,0:T(8,128)(2,1)S(1)}, s32[27,8,128]{2,1,0:T(8,128)S(1)}, s32[27,8,1...) custom-call(f32[8,128]{1,0:T(8,128)} %bitcast.18, s32[3,1,128]{2,1,0:T(1,128)} %bitcast.19, ...), custom_call_target="tpu_custom_call" | custom-call | tf_op jit(solution)/shard_map/flow/pallas_call | solution.py:445
  32.2 8.8 %conv.1 = (f32[8,256]{1,0:T(8,128)}, bf16[96,1024]{1,0:T(8,128)(2,1)}) custom-call(f32[32,2,128]{2,1,0:T(2,128)S(1)} %get-tuple-element.11.x_ref, f32[8,128]{1,0:T(8,128)S(1)} %get-tuple-element.12.nb_ref, bf16[2592,768]{1,0:T(8,128)(2,1)S(1)} %get-tuple-element.13.wt, s32[27,8,128]{2,1,0:T(8,128)S(1)} %get-tuple-element.14.spot_ref, ...), custom_call_target="tpu_custom_call" | custom-call | tf_op jit(solution)/shard_map/conv/pallas_call | solution.py:494

commit v8 on v7

--- a/solution.py
+++ b/solution.py
@@ -75,9 +75,9 @@
     wout_hbm, wt_hbm, km_hbm,
     x_ref, nb_ref, wt_ref, spot_ref, chunk_ref, near_ref, far_ref,
     lat_ref, coord_ref, own_ref, mod_ref, inp_ref, gain_ref, head_ref, bb_ref, tabh, tabl, wqkv, wout, km_ref,
-    gath, stage, scaled, bkt, bv, umat, hid_ref, ft_ref, fs_ref, p_ref, acc, hp_high, hp_low, hp_const, vel_ref, vel_in,
+    gath, stage, scaled, bkt, bv, umat, hid_ref, ft_ref, fs_ref, p_ref, acc, hp_high, hp_low, hp_const, ranked, dispatch,
     sendbuf, rbuf,
-    lsem, gs_sem, gr_sem, ps_sem, pr_sem, as_sem, ar_sem,
+    lsem, gs_sem, gr_sem, as_sem, ar_sem,
 ):
     me = lax.axis_index("seq")
     pair = lax.axis_index("pair")
@@ -145,6 +145,16 @@
     pl.semaphore_wait(barrier, N_SEQ)
     for dx, dz in NEAR_FIRST:
         g_copy(dx, dz).start()
+
+    own_rows = jnp.broadcast_to(own_ref[...], (TOK, TOK)).astype(F32)
+    own_cols = own_rows.T
+    earlier = (own_rows == own_cols) & (iota((TOK, TOK), 0) < iota((TOK, TOK), 1))
+    rank = jnp.sum(jnp.where(earlier, 1.0, 0.0), axis=0, keepdims=True)
+    ranked[...] = jnp.where(rank == ((iota((TOK, TOK), 0) // LAT) % CAP).astype(F32), 1.0, 0.0)
+    own96 = jnp.broadcast_to(own_ref[...], (3 * N_SEQ, TOK))
+    owner = iota((3 * N_SEQ, TOK), 0)
+    owner = jnp.where(owner < N_SEQ, owner, jnp.where(owner < 2 * N_SEQ, owner - N_SEQ - 1, owner - 2 * N_SEQ + 1))
+    dispatch[...] = jnp.where(own96 == owner, 1.0, 0.0).astype(BF16)
 
     scale1 = 1.0 + mod_ref[1]
     normed = (center * lax.rsqrt(variance + EPSILON) * scale1 + mod_ref[0]).astype(BF16)
@@ -253,43 +263,39 @@
         velocity = velocity + (mm_nt(hp_high[:, columns], c_high)
                                + (mm_nt(hp_high[:, columns], c_low) + mm_nt(hp_low[:, columns], c_high)))
     inv_dev = jnp.broadcast_to(lax.rsqrt(square * (1.0 / D) + EPSILON), (TOK, TOK)).T[0:1, :]
-    vel_ref[...] = velocity * inv_dev + hp_const[...]
-    swap = pltpu.make_async_remote_copy(
-        src_ref=vel_ref, dst_ref=vel_in, send_sem=ps_sem, recv_sem=pr_sem,
-        device_id={"pair": other}, device_id_type=mesh_ids)
-    swap.start()
-
-    own_rows = jnp.broadcast_to(own_ref[...], (TOK, TOK)).astype(F32)
-    own_cols = own_rows.T
-    earlier = (own_rows == own_cols) & (iota((TOK, TOK), 0) < iota((TOK, TOK), 1))
-    rank = jnp.sum(jnp.where(earlier, 1.0, 0.0), axis=0, keepdims=True)
-    ranked = rank == ((iota((TOK, TOK), 0) // LAT) % CAP).astype(F32)
-    own96 = jnp.broadcast_to(own_ref[...], (3 * N_SEQ, TOK))
-    owner = iota((3 * N_SEQ, TOK), 0)
-    owner = jnp.where(owner < N_SEQ, owner, jnp.where(owner < 2 * N_SEQ, owner - N_SEQ - 1, owner - 2 * N_SEQ + 1))
-    dispatch = jnp.where(own96 == owner, 1.0, 0.0).astype(BF16)
-    for dx, dz in NEAR_FIRST:
-        g_copy(dx, dz).wait_send()
-    swap.wait()
-    mine, theirs = vel_ref[...], vel_in[...]
+    velocity = velocity * inv_dev + hp_const[...]
+
     is_cond = pair == 0
-    cond = jnp.where(is_cond, mine, theirs)
-    uncond = jnp.where(is_cond, theirs, mine)
-    clean = lat_ref[...] - step_ref[0] * (uncond + GUIDANCE * (cond - uncond))
-    wide = jnp.where(ranked, jnp.concatenate([clean] * (TOK // LAT), axis=0), 0.0)
+    share = jnp.where(is_cond, 1.0, 0.0) * lat_ref[...] + (
+        step_ref[0] * jnp.where(is_cond, -GUIDANCE, GUIDANCE - 1.0)) * velocity
+    wide = jnp.concatenate([share] * (TOK // LAT), axis=0) * ranked[...]
     wide_high, wide_low = split(wide)
-    packed = mm_nt(dispatch, wide_high) + mm_nt(dispatch, wide_low)
+    packed = mm_nt(dispatch[...], wide_high) + mm_nt(dispatch[...], wide_low)
     sendbuf[:, 0, :] = jnp.where(
         iota((N_SEQ, TOK), 1) < LAT * CAP, packed[0:N_SEQ, :], packed[N_SEQ : 2 * N_SEQ, :])
     sendbuf[:, 1, :] = packed[2 * N_SEQ :, :]
 
-    for shift in range(1, N_SEQ):
-        dest = (me + shift) % N_SEQ
-        pltpu.make_async_remote_copy(
-            src_ref=sendbuf.at[dest], dst_ref=rbuf.at[me], send_sem=as_sem.at[shift], recv_sem=ar_sem.at[shift],
-            device_id={"seq": dest}, device_id_type=mesh_ids).start()
-    keep = pltpu.make_async_copy(sendbuf.at[me], rbuf.at[me], lsem.at[14])
+    def a_copy(core, dx, dz):
+        dest = ahead(dx, dz)
+        return pltpu.make_async_remote_copy(
+            src_ref=sendbuf.at[dest], dst_ref=rbuf.at[pair, me], send_sem=as_sem.at[core, dx, dz],
+            recv_sem=ar_sem.at[core, dx, dz], device_id={"pair": pair if core == 0 else other, "seq": dest},
+            device_id_type=mesh_ids)
+
+    def a_arrival(core, dx, dz):
+        source = behind(dx, dz)
+        return pltpu.make_async_remote_copy(
+            src_ref=sendbuf.at[source], dst_ref=rbuf.at[pair if core == 0 else other, source],
+            send_sem=as_sem.at[core, dx, dz], recv_sem=ar_sem.at[core, dx, dz], device_id={"seq": me},
+            device_id_type=mesh_ids)
+
+    far_first = [(core, dx, dz) for dx, dz in reversed(NEAR_FIRST) for core in range(2)] + [(1, 0, 0)]
+    for core, dx, dz in far_first:
+        a_copy(core, dx, dz).start()
+    keep = pltpu.make_async_copy(sendbuf.at[me], rbuf.at[pair, me], lsem.at[14])
     keep.start()
+    for dx, dz in NEAR_FIRST:
+        g_copy(dx, dz).wait_send()
 
     lower = jnp.maximum(me - 1, 0)
     upper = jnp.minimum(me + 1, N_SEQ - 1)
@@ -305,12 +311,9 @@
     far_ref[...] = jnp.where(index >= SLOTS, jnp.minimum(index - SLOTS, 300), 300).astype(F32)
     loads[13].wait()
     keep.wait()
-    for shift in range(1, N_SEQ):
-        source = (me + N_SEQ - shift) % N_SEQ
-        pltpu.make_async_remote_copy(
-            src_ref=sendbuf.at[source], dst_ref=rbuf.at[source], send_sem=as_sem.at[shift], recv_sem=ar_sem.at[shift],
-            device_id={"seq": me}, device_id_type=mesh_ids).wait()
-    x_ref[...] = rbuf[...]
+    for core, dx, dz in far_first:
+        a_arrival(core, dx, dz).wait()
+    x_ref[...] = rbuf[0] + rbuf[1]
 
 
 TRIPLE = 3
@@ -477,11 +480,11 @@
             pltpu.VMEM((LAT, D), BF16),
             pltpu.VMEM((LAT, D), BF16),
             pltpu.VMEM((LAT, TOK), F32),
-            pltpu.VMEM((LAT, TOK), F32),
-            pltpu.VMEM((LAT, TOK), F32),
+            pltpu.VMEM((TOK, TOK), F32),
+            pltpu.VMEM((3 * N_SEQ, TOK), BF16),
             pltpu.VMEM((N_SEQ, 2, TOK), F32),
-            pltpu.VMEM((N_SEQ, 2, TOK), F32),
-            dma((15,)), dma((NX, NZ)), dma((NX, NZ)), dma, dma, dma((N_SEQ,)), dma((N_SEQ,)),
+            pltpu.VMEM((2, N_SEQ, 2, TOK), F32),
+            dma((15,)), dma((NX, NZ)), dma((NX, NZ)), dma((2, NX, NZ)), dma((2, NX, NZ)),
         ],
         compiler_params=pltpu.CompilerParams(collective_id=0, has_side_effects=True, vmem_limit_bytes=40 << 20),
         name="flow",

time: 41.1 us -> 41.5 us (level)
  Pallas kernels: 39.6 us -> 40.1 us
    pallas_call x1, Pallas kernels: 30.9 us -> 31.3 us  [per_device(): pl.pallas_call(flow_kernel, out_shape=(jax.ShapeDtypeStruct((N_SEQ, 2, TO...]
where the time goes in v8:
time: 41.5 us; the launch traced here: 41.3 us
  Pallas kernels  40.1 us (97%)
  between operations  1.29 us (3%)
    pallas_call x1, Pallas kernels, per_device(): pl.pallas_call(flow_kernel, out_shape=(jax.ShapeDtypeStruct((N_SEQ, 2, TO...  31.3 us
    pallas_call x1, Pallas kernels, per_device(): pl.pallas_call(conv_kernel, out_shape=(jax.ShapeDtypeStruct((LAT, SLOTS),...  8.77 us

profile of v8, /device:TPU:1, one launch (start us, length us, event | category | flops | bytes accessed | tf_op | source)
XLA Modules:
  0.0 41.3 jit_solution(10077461043948906190)
XLA Ops:
  1.3 31.3 %flow.1 = (f32[32,2,128]{2,1,0:T(2,128)S(1)}, f32[8,128]{1,0:T(8,128)S(1)}, bf16[2592,768]{1,0:T(8,128)(2,1)S(1)}, s32[27,8,128]{2,1,0:T(8,128)S(1)}, s32[27,8,1...) custom-call(f32[8,128]{1,0:T(8,128)} %bitcast.18, s32[3,1,128]{2,1,0:T(1,128)} %bitcast.19, ...), custom_call_target="tpu_custom_call" | custom-call | tf_op jit(solution)/shard_map/flow/pallas_call | solution.py:448
  32.6 8.8 %conv.1 = (f32[8,256]{1,0:T(8,128)}, bf16[96,1024]{1,0:T(8,128)(2,1)}) custom-call(f32[32,2,128]{2,1,0:T(2,128)S(1)} %get-tuple-element.11.x_ref, f32[8,128]{1,0:T(8,128)S(1)} %get-tuple-element.12.nb_ref, bf16[2592,768]{1,0:T(8,128)(2,1)S(1)} %get-tuple-element.13.wt, s32[27,8,128]{2,1,0:T(8,128)S(1)} %get-tuple-element.14.spot_ref, ...), custom_call_target="tpu_custom_call" | custom-call | tf_op jit(solution)/shard_map/conv/pallas_call | solution.py:497

commit v9 on v8

--- a/solution.py
+++ b/solution.py
@@ -72,9 +72,9 @@
 
 def flow_kernel(
     lat_hbm, coord_hbm, own_hbm, step_ref, mod_hbm, inp_hbm, gain_hbm, head_hbm, bb_hbm, tabh_hbm, tabl_hbm, wqkv_hbm,
-    wout_hbm, wt_hbm, km_hbm,
-    x_ref, nb_ref, wt_ref, spot_ref, chunk_ref, near_ref, far_ref,
-    lat_ref, coord_ref, own_ref, mod_ref, inp_ref, gain_ref, head_ref, bb_ref, tabh, tabl, wqkv, wout, km_ref,
+    wout_hbm, wt_hbm, km_hbm, dproj_hbm,
+    x_ref, pick_ref, wt_ref, spot_ref, chunk_ref, near_ref, far_ref, dh_ref, dl_ref,
+    lat_ref, coord_ref, own_ref, mod_ref, inp_ref, gain_ref, head_ref, bb_ref, tabh, tabl, wqkv, wout, km_ref, dproj_ref,
     gath, stage, scaled, bkt, bv, umat, hid_ref, ft_ref, fs_ref, p_ref, acc, hp_high, hp_low, hp_const, ranked, dispatch,
     sendbuf, rbuf,
     lsem, gs_sem, gr_sem, as_sem, ar_sem,
@@ -97,7 +97,7 @@
         for number, (source, target) in enumerate((
             (lat_hbm, lat_ref), (coord_hbm, coord_ref), (own_hbm, own_ref), (mod_hbm, mod_ref), (inp_hbm, inp_ref),
             (gain_hbm, gain_ref), (head_hbm, head_ref), (bb_hbm, bb_ref), (tabh_hbm, tabh), (tabl_hbm, tabl),
-            (wqkv_hbm, wqkv), (wout_hbm, wout), (km_hbm, km_ref), (wt_hbm, wt_ref)))
+            (wqkv_hbm, wqkv), (wout_hbm, wout), (km_hbm, km_ref), (wt_hbm, wt_ref), (dproj_hbm, dproj_ref)))
     ]
     for load in loads[:12]:
         load.start()
@@ -180,8 +180,8 @@
     head_scaled = head_ref[...] * (1.0 + mod_ref[4])
     hp_high[...], hp_low[...] = split(head_scaled)
     hp_const[...] = jnp.broadcast_to(jnp.sum(head_ref[...] * mod_ref[3], axis=1, keepdims=True), (LAT, TOK))
-    loads[12].start()
-    loads[13].start()
+    for load in loads[12:]:
+        load.start()
 
     def features(number):
         sources = []
@@ -292,16 +292,25 @@
     far_first = [(core, dx, dz) for dx, dz in reversed(NEAR_FIRST) for core in range(2)] + [(1, 0, 0)]
     for core, dx, dz in far_first:
         a_copy(core, dx, dz).start()
-    keep = pltpu.make_async_copy(sendbuf.at[me], rbuf.at[pair, me], lsem.at[14])
+    keep = pltpu.make_async_copy(sendbuf.at[me], rbuf.at[pair, me], lsem.at[15])
     keep.start()
     for dx, dz in NEAR_FIRST:
         g_copy(dx, dz).wait_send()
 
     lower = jnp.maximum(me - 1, 0)
     upper = jnp.minimum(me + 1, N_SEQ - 1)
-    nb_ref[0:1, :] = gath[lower].astype(F32)[11:12, :]
-    nb_ref[1:2, :] = gath[upper].astype(F32)[11:12, :]
-    nb_ref[2:8, :] = jnp.zeros((6, TOK), F32)
+    sub = iota((HALO, TOK), 0)
+    lane = iota((HALO, TOK), 1)
+    for side, neighbour in ((0, lower), (1, upper)):
+        blocks = jnp.broadcast_to(gath[neighbour].astype(F32)[11:12, :], (HALO, TOK))
+        first = 8 if side == 0 else 0
+        chosen = jnp.sum(jnp.where(lane == sub // BLK + first, blocks, 0.0), axis=1, keepdims=True)
+        source = chosen * (BLK // CAP) + ((iota((HALO, 1), 0) % BLK) // CAP).astype(F32)
+        pick_ref[side] = jnp.where(iota((HALO, N_SEQ), 1).astype(F32) == source, 1.0, 0.0).astype(BF16)
+    loads[14].wait()
+    d_high, d_low = split(dproj_ref[...])
+    dh_ref[...] = jnp.concatenate([d_high.astype(F32)] * (TOK // LAT), axis=0).astype(BF16)
+    dl_ref[...] = jnp.concatenate([d_low.astype(F32)] * (TOK // LAT), axis=0).astype(BF16)
     loads[12].wait()
     index = km_ref[...]
     index = jnp.where(index < SLOTS, ((index & (CAP - 1)) << 5) + (index >> 3), index)
@@ -323,11 +332,9 @@
 
 
 def conv_kernel(
-    x_ref, nb_ref, wt, spot_ref, chunk_ref, near_ref, far_ref, dproj_hbm, owned_ref, dec_ref, dproj_ref, feats, prod_a,
-    prod_b, acc_x, acc_m, lsem
+    x_ref, pick_ref, wt, spot_ref, chunk_ref, near_ref, far_ref, dh_ref, dl_ref, owned_ref, dec_ref, feats, prod_a,
+    prod_b, acc_x, acc_m
 ):
-    load = pltpu.make_async_copy(dproj_hbm, dproj_ref, lsem)
-    load.start()
     x0 = x_ref[:, 0, :]
     x1 = x_ref[:, 1, :]
 
@@ -346,20 +353,13 @@
     lane = iota((HALO, TOK), 1)
     parts = [own_rows]
     for side, x_side in ((0, x0), (1, x1)):
-        blocks = jnp.broadcast_to(nb_ref[side : side + 1, :], (HALO, TOK))
-        first = 8 if side == 0 else 0
-        chosen = jnp.sum(jnp.where(lane == sub // BLK + first, blocks, 0.0), axis=1, keepdims=True)
-        source = chosen * (BLK // CAP) + ((iota((HALO, 1), 0) % BLK) // CAP).astype(F32)
-        pick = jnp.where(iota((HALO, N_SEQ), 1).astype(F32) == source, 1.0, 0.0).astype(BF16)
+        pick = pick_ref[side]
         x_high, x_low = split(x_side)
         rows = mm(pick, x_high) + mm(pick, x_low)
         offset = CAP if side == 0 else 0
         parts.append(jnp.where(lane // LAT == sub % CAP + offset, rows, 0.0))
     l_high, l_low = split(jnp.concatenate(parts, axis=0))
-    load.wait()
-    p_high, p_low = split(dproj_ref[...])
-    p_high = jnp.concatenate([p_high.astype(F32)] * (TOK // LAT), axis=0).astype(BF16)
-    p_low = jnp.concatenate([p_low.astype(F32)] * (TOK // LAT), axis=0).astype(BF16)
+    p_high, p_low = dh_ref[...], dl_ref[...]
     value = mm(jnp.concatenate([l_high, l_low], axis=1), jnp.concatenate([p_high, p_high], axis=0)) + mm(l_high, p_low)
     half = value * 0.5
     feats[...] = (half * jnp.tanh(half) + half).astype(BF16)
@@ -448,10 +448,11 @@
     handed = pl.pallas_call(
         flow_kernel,
         out_shape=(
-            jax.ShapeDtypeStruct((N_SEQ, 2, TOK), F32), jax.ShapeDtypeStruct((8, TOK), F32),
-            jax.ShapeDtypeStruct((KOFF * OUT_DEV, DEC), BF16), conv_table, conv_table, conv_row, conv_row),
-        in_specs=hbm(3) + [pl.BlockSpec(memory_space=pltpu.SMEM)] + hbm(11),
-        out_specs=tuple(vmem(7)),
+            jax.ShapeDtypeStruct((N_SEQ, 2, TOK), F32), jax.ShapeDtypeStruct((2, HALO, N_SEQ), BF16),
+            jax.ShapeDtypeStruct((KOFF * OUT_DEV, DEC), BF16), conv_table, conv_table, conv_row, conv_row,
+            jax.ShapeDtypeStruct((TOK, DEC), BF16), jax.ShapeDtypeStruct((TOK, DEC), BF16)),
+        in_specs=hbm(3) + [pl.BlockSpec(memory_space=pltpu.SMEM)] + hbm(12),
+        out_specs=tuple(vmem(9)),
         scratch_shapes=[
             pltpu.VMEM((LAT, TOK), F32),
             pltpu.VMEM((3, 1, TOK), jnp.int32),
@@ -466,6 +467,7 @@
             pltpu.VMEM((D, 3 * HW), BF16),
             pltpu.VMEM((HW, D), BF16),
             pltpu.VMEM((KOFF, BLOCKS, TOK), jnp.int32),
+            pltpu.VMEM((LAT, DEC), F32),
             pltpu.VMEM((N_SEQ, 16, TOK), BF16),
             pltpu.VMEM((16, TOK), F32),
             pltpu.VMEM((FEAT, D), BF16),
@@ -484,7 +486,7 @@
             pltpu.VMEM((3 * N_SEQ, TOK), BF16),
             pltpu.VMEM((N_SEQ, 2, TOK), F32),
             pltpu.VMEM((2, N_SEQ, 2, TOK), F32),
-            dma((15,)), dma((NX, NZ)), dma((NX, NZ)), dma((2, NX, NZ)), dma((2, NX, NZ)),
+            dma((16,)), dma((NX, NZ)), dma((NX, NZ)), dma((2, NX, NZ)), dma((2, NX, NZ)),
         ],
         compiler_params=pltpu.CompilerParams(collective_id=0, has_side_effects=True, vmem_limit_bytes=40 << 20),
         name="flow",
@@ -492,25 +494,23 @@
         latents[0], jnp.transpose(voxel_coords, (1, 0, 2)), owner_map.reshape(1, TOK)), step_time, *in_hbm(
         modulation.reshape(5, 1, D), in_proj, norm_gain, head_proj.T, border_blocks[0, 0], jnp.asarray(table_high),
         jnp.asarray(table_low), qkv_proj, out_proj,
-        jnp.swapaxes(conv_weight, 1, 2).reshape(KOFF * OUT_DEV, DEC), kernel_map.reshape(KOFF, BLOCKS, TOK)),
+        jnp.swapaxes(conv_weight, 1, 2).reshape(KOFF * OUT_DEV, DEC), kernel_map.reshape(KOFF, BLOCKS, TOK), decoder_projection),
     )
     owned, decoded = pl.pallas_call(
         conv_kernel,
         out_shape=(jax.ShapeDtypeStruct((LAT, SLOTS), F32), jax.ShapeDtypeStruct((OUT_DEV, FINE), BF16)),
-        in_specs=vmem(7) + hbm(1),
+        in_specs=vmem(9),
         out_specs=tuple(vmem(2)),
         scratch_shapes=[
-            pltpu.VMEM((LAT, DEC), F32),
             pltpu.VMEM((2 * SLOTS, DEC), BF16),
             pltpu.VMEM((TRIPLE * OUT_DEV, 2 * SLOTS), F32),
             pltpu.VMEM((TRIPLE * OUT_DEV, 2 * SLOTS), F32),
             pltpu.VMEM((OUT_DEV, FINE), F32),
             pltpu.VMEM((OUT_DEV, FINE), F32),
-            dma,
         ],
         compiler_params=pltpu.CompilerParams(vmem_limit_bytes=40 << 20),
         name="conv",
-    )(*handed, *in_hbm(decoder_projection))
+    )(*handed)
     return owned[None, None], decoded.T[None, None]
 
 

time: 41.5 us -> 40.5 us (0.976)
  Pallas kernels: 40.1 us -> 39.1 us
    pallas_call x1, Pallas kernels: 8.77 us -> 7.83 us  [per_device(): pl.pallas_call(conv_kernel, out_shape=(jax.ShapeDtypeStruct((LAT, SLOTS),...]
where the time goes in v9:
time: 40.5 us; the launch traced here: 40.4 us
  Pallas kernels  39.1 us (97%)
  between operations  1.29 us (3%)
    pallas_call x1, Pallas kernels, per_device(): pl.pallas_call(flow_kernel, out_shape=(jax.ShapeDtypeStruct((N_SEQ, 2, TO...  31.3 us
    pallas_call x1, Pallas kernels, per_device(): pl.pallas_call(conv_kernel, out_shape=(jax.ShapeDtypeStruct((LAT, SLOTS),...  7.83 us

profile of v9, /device:TPU:1, one launch (start us, length us, event | category | flops | bytes accessed | tf_op | source)
XLA Modules:
  0.0 40.4 jit_solution(12431881641716431909)
XLA Ops:
  1.3 31.3 %flow.1 = (f32[32,2,128]{2,1,0:T(2,128)S(1)}, bf16[2,128,32]{2,1,0:T(8,128)(2,1)S(1)}, bf16[2592,768]{1,0:T(8,128)(2,1)S(1)}, s32[27,8,128]{2,1,0:T(8,128)S(1)},...) custom-call(f32[8,128]{1,0:T(8,128)} %bitcast.18, ...), custom_call_target="tpu_custom_call" | custom-call | tf_op jit(solution)/shard_map/flow/pallas_call | solution.py:448
  32.6 7.8 %conv.1 = (f32[8,256]{1,0:T(8,128)}, bf16[96,1024]{1,0:T(8,128)(2,1)}) custom-call(f32[32,2,128]{2,1,0:T(2,128)S(1)} %get-tuple-element.13.x_ref, bf16[2,128,32]{2,1,0:T(8,128)(2,1)S(1)} %get-tuple-element.14.pick_ref, bf16[2592,768]{1,0:T(8,128)(2,1)S(1)} %get-tuple-element.15.wt, s32[27,8,128]{2,1,0:T(8,128)S(1)} %get-tuple-element.16.spot_ref, ...), custom_call_target="tpu_custom_call" | custom-call | tf_op jit(solution)/shard_map/conv/pallas_call | solution.py:499

commit v10 on v9

--- a/solution.py
+++ b/solution.py
@@ -142,10 +142,6 @@
             src_ref=gath.at[me], dst_ref=gath.at[me], send_sem=gs_sem.at[dx, dz], recv_sem=gr_sem.at[dx, dz],
             device_id={"seq": ahead(dx, dz)}, device_id_type=mesh_ids)
 
-    pl.semaphore_wait(barrier, N_SEQ)
-    for dx, dz in NEAR_FIRST:
-        g_copy(dx, dz).start()
-
     own_rows = jnp.broadcast_to(own_ref[...], (TOK, TOK)).astype(F32)
     own_cols = own_rows.T
     earlier = (own_rows == own_cols) & (iota((TOK, TOK), 0) < iota((TOK, TOK), 1))
@@ -176,6 +172,11 @@
         both = queries[:, columns]
         mine = jnp.concatenate([jnp.where(first_half, both, 0.0), jnp.where(first_half, 0.0, both)], axis=0)
         umat[two * 256 : (two + 1) * 256, :] = mm(mine.astype(BF16), bkt[columns, :]).astype(BF16)
+
+    pl.semaphore_wait(barrier, N_SEQ)
+    for dx, dz in NEAR_FIRST:
+        g_copy(dx, dz).start()
+
     bv[...] = mm(scaled[...], wqkv[:, 2 * HW : 3 * HW]).astype(BF16)
     head_scaled = head_ref[...] * (1.0 + mod_ref[4])
     hp_high[...], hp_low[...] = split(head_scaled)

time: 40.5 us -> 40.5 us (level)
  no operation moved by 1% of the time
where the time goes in v10:
time: 40.5 us; the launch traced here: 40.4 us
  Pallas kernels  39.1 us (97%)
  between operations  1.29 us (3%)
    pallas_call x1, Pallas kernels, per_device(): pl.pallas_call(flow_kernel, out_shape=(jax.ShapeDtypeStruct((N_SEQ, 2, TO...  31.3 us
    pallas_call x1, Pallas kernels, per_device(): pl.pallas_call(conv_kernel, out_shape=(jax.ShapeDtypeStruct((LAT, SLOTS),...  7.83 us

profile of v10, /device:TPU:1, one launch (start us, length us, event | category | flops | bytes accessed | tf_op | source)
XLA Modules:
  0.0 40.4 jit_solution(2144088996815079102)
XLA Ops:
  1.3 31.3 %flow.1 = (f32[32,2,128]{2,1,0:T(2,128)S(1)}, bf16[2,128,32]{2,1,0:T(8,128)(2,1)S(1)}, bf16[2592,768]{1,0:T(8,128)(2,1)S(1)}, s32[27,8,128]{2,1,0:T(8,128)S(1)},...) custom-call(f32[8,128]{1,0:T(8,128)} %bitcast.18, ...), custom_call_target="tpu_custom_call" | custom-call | tf_op jit(solution)/shard_map/flow/pallas_call | solution.py:449
  32.6 7.8 %conv.1 = (f32[8,256]{1,0:T(8,128)}, bf16[96,1024]{1,0:T(8,128)(2,1)}) custom-call(f32[32,2,128]{2,1,0:T(2,128)S(1)} %get-tuple-element.13.x_ref, bf16[2,128,32]{2,1,0:T(8,128)(2,1)S(1)} %get-tuple-element.14.pick_ref, bf16[2592,768]{1,0:T(8,128)(2,1)S(1)} %get-tuple-element.15.wt, s32[27,8,128]{2,1,0:T(8,128)S(1)} %get-tuple-element.16.spot_ref, ...), custom_call_target="tpu_custom_call" | custom-call | tf_op jit(solution)/shard_map/conv/pallas_call | solution.py:500
